TPU v7x, 32 devices: a whole 2x2x4 slice. The times are simulated.
32 devices in a mesh: bx: 8 (over y, x, core), by: 4 (over z).
Axes of the slice: x: 2, y: 2, z: 4, core: 2. Of those that a mesh axis runs over, the one named last changes fastest.
Arguments:
- right_sides: float32 [8, 4, 128, 768], P('bx', 'by'), may hold values from -6 to 6
- skeleton_order: int32 [8, 4, 4, 768], P('bx', 'by'), may hold values from 0 to 767, as said below
- interp_first: float32 [8, 4, 384, 384], P('bx', 'by'), may hold values from -0.15625 to 0.15625
- interp_second: float32 [8, 4, 384, 192], P('bx', 'by'), may hold values from -0.15625 to 0.15625
- interp_third: float32 [8, 4, 384, 96], P('bx', 'by'), may hold values from -0.15625 to 0.15625
- interp_fourth: float32 [8, 4, 384, 48], P('bx', 'by'), may hold values from -0.15625 to 0.15625
- inverse_first: float32 [8, 4, 384, 384], P('bx', 'by'), may hold values from -0.25 to 0.25
- inverse_second: float32 [8, 4, 384, 192], P('bx', 'by'), may hold values from -0.25 to 0.25
- inverse_third: float32 [8, 4, 384, 96], P('bx', 'by'), may hold values from -0.25 to 0.25
- inverse_fourth: float32 [8, 4, 384, 48], P('bx', 'by'), may hold values from -0.25 to 0.25
- couple_first: float32 [8, 4, 5, 384, 384], P('bx', 'by'), may hold values from -0.09375 to 0.09375
- couple_second: float32 [8, 4, 5, 384, 192], P('bx', 'by'), may hold values from -0.09375 to 0.09375
- couple_third: float32 [8, 4, 5, 384, 96], P('bx', 'by'), may hold values from -0.09375 to 0.09375
- couple_fourth: float32 [8, 4, 5, 384, 48], P('bx', 'by'), may hold values from -0.09375 to 0.09375
- root_inverse: float32 [8, 4, 384, 48], P('bx', 'by'), may hold values from -0.21875 to 0.21875
Outputs:
- solution: float32 [8, 4, 128, 768], P('bx', 'by')
Inputs may be any that keep to these rules, and one draw needn't show every extreme that they name: For every fine box and level l, skeleton_order[i, j, l, :] is a permutation of 0 to 767, the same at all fine boxes of one level-l box.
All inputs are finite; a program needn't handle non-finite values.
Results may differ from a plain program's by a relative error of at most 0.0003.
Values sent between devices are 32-bit elements; how exact they have to be, the bound alone decides.
A program may use at most 128 MiB of HBM per device.

v0:
```python
import functools

import jax
import jax.numpy as jnp
from jax import lax
from jax.experimental import pallas as pl
from jax.experimental.pallas import tpu as pltpu
from jax.sharding import PartitionSpec as P

REACH = ((1, 1), (1, 2), (2, 2), (2, 4))
F32 = jnp.float32
BF16 = jnp.bfloat16
MESH = pl.DeviceIdType.MESH
NN = (((1,), (0,)), ((), ()))
TN = (((0,), (0,)), ((), ()))
NT = (((1,), (1,)), ((), ()))


def halves(x):
    high = x.astype(BF16)
    return high, (x - high.astype(F32)).astype(BF16)


def product(a, b, dims):
    return lax.dot_general(a, b, dims, preferred_element_type=F32)


def dot3(a, b, dims):
    ah, al = halves(a)
    bh, bl = halves(b)
    return product(ah, bh, dims) + (product(ah, bl, dims) + product(al, bh, dims))


def pick_left(onehot, b, dims):
    bh, bl = halves(b)
    return product(onehot, bh, dims) + product(onehot, bl, dims)


def flips(m):
    return (m >> 1) & 1, (m & 1) | ((m >> 2 & 1) << 1)


def kernel(size_x, size_y, *refs):
    (rhs, order_col, order_row, t0, t1, t2, t3, g0, g1, g2, g3, k0, k1, k2, k3, root, out) = refs[:17]
    (ybuf, vbuf, qsend, qrecv, urecv1, urecv2, urecv3, xrecv1, xrecv2, xrecv3, xpart, tg1, tg2, tg3,
     n0, n1, n2, n3, abuf, ypart, tpart, ssend, ptbuf, send, recv) = refs[17:]
    interps, inverses, couples = (t0, t1, t2, t3), (g0, g1, g2, g3), (k0, k1, k2, k3)
    urecvs = (None, urecv1, urecv2, urecv3)
    xrecvs = (None, xrecv1, xrecv2, xrecv3)
    tgs = (None, tg1, tg2, tg3)
    ns = (n0, n1, n2, n3)
    skel = t0.shape[2]
    box = 2 * skel
    i, j = lax.axis_index("bx"), lax.axis_index("by")
    bits = (lax.rem(j, 2), lax.rem(i, 2), lax.rem(lax.div(j, 2), 2))
    ranks = [jnp.int32(0), bits[0], bits[0] + 2 * bits[1], bits[0] + 2 * bits[1] + 4 * bits[2]]

    def toggled(value, mask):
        for b in (0, 1):
            if mask >> b & 1:
                value = value + (1 << b) * (1 - 2 * lax.rem(lax.div(value, 1 << b), 2))
        return value

    def member(m):
        mx, my = flips(m)
        return (toggled(i, mx), toggled(j, my))

    def rank_of(level, m):
        rank = jnp.int32(0)
        for b in range(level):
            bit = bits[b]
            rank = rank + (1 << b) * ((1 - bit) if m >> b & 1 else bit)
        return rank

    count = [0]

    def slot():
        count[0] += 1
        return count[0] - 1

    def neighbour(level, k):
        rx, ry = REACH[level]
        bx, by = lax.div(i, rx), lax.div(j, ry)
        if k == 1:
            return i >= rx, (i - rx, j)
        if k == 2:
            return i + rx < size_x, (i + rx, j)
        if k == 3:
            return j >= ry, (i, j - ry)
        return j + ry < size_y, (i, j + ry)

    opposite = {1: 2, 2: 1, 3: 4, 4: 3}
    level_has = [[k for k in (1, 2, 3, 4) if (REACH[l][0] < size_x if k < 3 else REACH[l][1] < size_y)] for l in range(4)]

    def rcopy(src, dst, s, dev):
        return pltpu.make_async_remote_copy(src, dst, send.at[s], recv.at[s], device_id=dev, device_id_type=MESH)

    for level in range(4):
        for k in (1, 2, 3, 4):
            there, _ = neighbour(level, k)

            @pl.when(jnp.logical_not(there))
            def _():
                ybuf[level, pl.ds(k * skel, skel), :] = jnp.zeros((skel, ybuf.shape[2]), F32)
                qrecv[level, k - 1] = jnp.zeros((skel, ybuf.shape[2]), F32)

    barrier = pltpu.get_barrier_semaphore()
    for m in range(1, 8):
        pl.semaphore_signal(barrier, 1, device_id=member(m), device_id_type=MESH)
    total = jnp.int32(7)
    greeted = set()
    for level in range(4):
        for k in level_has[level]:
            key = (k, REACH[level][0] if k < 3 else REACH[level][1])
            if key in greeted:
                continue
            greeted.add(key)
            there, dev = neighbour(level, k)

            @pl.when(there)
            def _():
                pl.semaphore_signal(barrier, 1, device_id=dev, device_id_type=MESH)
            total = total + there.astype(jnp.int32)
    pl.semaphore_wait(barrier, total)

    pending = []

    t_copies = [[], [], [], []]

    def send_interp(level):
        for m in [m for m in range(1, 1 << level) if not m & 2]:
            c = rcopy(interps[level].at[0, 0], tgs[level].at[ranks[level]], slot(), member(m))
            c.start()
            t_copies[level].append(c)
            pending.append(c)

    send_interp(1)

    def make_n(level):
        own = inverses[level][0, 0]
        cols = own.shape[1]
        if level == 0:
            acc = dot3(interps[0][0, 0], own, NN)
        else:
            tgs[level][ranks[level]] = interps[level][0, 0]
            for c in t_copies[level]:
                c.wait_recv()
            shared = []
            for m in [m for m in range(1 << level) if not m & 2 and level > 1]:
                block = rank_of(level, m)
                held = interps[level].at[0, 0] if m == 0 else tgs[level].at[block]
                c = rcopy(held, tgs[level].at[block], slot(), member(2))
                c.start()
                shared.append(c)
                pending.append(c)
            for c in shared:
                c.wait_recv()
            acc = jnp.zeros((skel, cols), F32)
            for q in range(1 << level):
                acc = acc + dot3(tgs[level][q], inverses[level][0, 0, q * cols:(q + 1) * cols, :], NN)
        ns[level][:skel, :] = -acc
        ns[level][skel:, :] = own

    def onehot_pt(level):
        lanes = lax.broadcasted_iota(jnp.int32, (box, box), 1)
        return jnp.where(lanes == order_col[:, level:level + 1], 1.0, 0.0).astype(BF16)

    def onehot_p(level):
        rows = lax.broadcasted_iota(jnp.int32, (box, box), 0)
        return jnp.where(rows == order_row[0, 0, level:level + 1, :], 1.0, 0.0).astype(BF16)

    for level in range(4):
        cols = interps[level].shape[3]
        rank = ranks[level]
        rows = pl.ds(pl.multiple_of(rank * cols, cols), cols)
        if level == 0:
            make_n(0)
            abuf[...] = pick_left(onehot_pt(0), rhs[0, 0], NT)
        else:
            abuf[...] = pick_left(ptbuf[...], vbuf[level - 1], NN)
        y_own = dot3(ns[level][...], abuf[...], TN)
        ypart[level, :cols, :] = y_own
        ybuf[level, rows, :] = y_own
        gathers = []
        for m in range(1, 1 << level):
            c = rcopy(ypart.at[level, pl.ds(0, cols), :], ybuf.at[level, rows, :], slot(), member(m))
            c.start()
            gathers.append(c)
            pending.append(c)
        for c in gathers:
            c.wait_recv()
        for k in level_has[level]:
            s = slot()
            far = opposite[k]
            there, dev = neighbour(level, k)
            c = rcopy(ybuf.at[level, pl.ds(0, skel), :], ybuf.at[level, pl.ds(far * skel, skel), :], s, dev)

            @pl.when(there)
            def _():
                c.start()
            pending.append((there, c))
        base = count[0] - len(level_has[level])
        if level < 2:
            send_interp(level + 2)
        if level < 3:
            make_n(level + 1)
            ptbuf[...] = onehot_pt(level + 1)
        for k in level_has[level]:
            there, dev = neighbour(level, k)
            sent_as = level_has[level].index(opposite[k])
            c = rcopy(ybuf.at[level, pl.ds(0, skel), :], ybuf.at[level, pl.ds(k * skel, skel), :], base + sent_as, dev)

            @pl.when(there)
            def _():
                c.wait_recv()
        coupling = couples[level][0, 0].reshape(5 * skel, cols)
        s_own = abuf[rows, :] - dot3(coupling, ybuf[level], TN)
        ssend[level, :cols, :] = s_own
        wide = min(level + 1, 3)
        spot = pl.ds(pl.multiple_of(ranks[wide] * cols, cols), cols)
        vbuf[level, spot, :] = s_own
        gathers = []
        for m in range(1, 1 << wide):
            c = rcopy(ssend.at[level, pl.ds(0, cols), :], vbuf.at[level, spot, :], slot(), member(m))
            c.start()
            gathers.append(c)
            pending.append(c)
        for c in gathers:
            c.wait_recv()

    t_own = dot3(root[0, 0], vbuf[3, :skel, :], TN)

    for level in (3, 2, 1, 0):
        cols = interps[level].shape[3]
        rank = ranks[level]
        members = 1 << level
        rows = pl.ds(pl.multiple_of(rank * cols, cols), cols)
        tpart[:cols, :] = t_own
        q = dot3(couples[level][0, 0].reshape(5 * skel, cols), t_own, NN)
        qsend[level] = q
        base = count[0]
        for k in level_has[level]:
            s = slot()
            there, dev = neighbour(level, k)
            c = rcopy(qsend.at[level, pl.ds(k * skel, skel), :], qrecv.at[level, opposite[k] - 1], s, dev)

            @pl.when(there)
            def _():
                c.start()
            pending.append((there, c))
        y_own = ypart[level, :cols, :]
        abuf[:skel, :] = -dot3(interps[level][0, 0], y_own, NN)
        abuf[skel:, :] = jnp.zeros_like(abuf[skel:, :])
        abuf[rows, :] = abuf[rows, :] + t_own
        rows_y = pl.ds(pl.multiple_of(skel + rank * cols, 8), cols)
        abuf[rows_y, :] = y_own
        ptbuf[...] = onehot_p(level) if level > 0 else onehot_pt(0)
        for k in level_has[level]:
            there, dev = neighbour(level, k)
            sent_as = level_has[level].index(opposite[k])
            c = rcopy(qsend.at[level, pl.ds(k * skel, skel), :], qrecv.at[level, k - 1], base + sent_as, dev)

            @pl.when(there)
            def _():
                c.wait_recv()
        u = q[:skel] + ((qrecv[level, 0] + qrecv[level, 1]) + (qrecv[level, 2] + qrecv[level, 3]))
        if level > 0:
            qsend[level, :skel, :] = u
            gathers = []
            for m in range(1, members):
                far_rows = pl.ds(pl.multiple_of(rank_of(level, m) * cols, cols), cols)
                c = rcopy(qsend.at[level, far_rows, :], urecvs[level].at[m - 1], slot(), member(m))
                c.start()
                gathers.append(c)
                pending.append(c)
            for c in gathers:
                c.wait_recv()
            u_own = qsend[level, rows, :]
            for m in range(1, members):
                u_own = u_own + urecvs[level][m - 1]
        else:
            u_own = u
        comb = -dot3(ns[level][...], u_own, NN)
        abuf[...] = abuf[...] + comb
        if level > 0:
            xpart[level] = pick_left(ptbuf[...], abuf[...], NN)
            size = box // members
            gathers = []
            for m in range(1, members):
                far_rows = pl.ds(pl.multiple_of(rank_of(level, m) * size, size), size)
                c = rcopy(xpart.at[level, far_rows, :], xrecvs[level].at[m - 1], slot(), member(m))
                c.start()
                gathers.append(c)
                pending.append(c)
            for c in gathers:
                c.wait_recv()
            t_own = xpart[level, pl.ds(pl.multiple_of(rank * size, size), size), :]
            for m in range(1, members):
                t_own = t_own + xrecvs[level][m - 1]
        else:
            ch, cl = halves(abuf[...])
            pt = ptbuf[...]
            out[0, 0] = product(ch, pt, TN) + product(cl, pt, TN)

    for item in pending:
        if isinstance(item, tuple):
            there, c = item

            @pl.when(there)
            def _():
                c.wait_send()
        else:
            item.wait_send()


def body(size_x, size_y, right_sides, skeleton_order, *weights):
    rows = right_sides.shape[2]
    box = right_sides.shape[3]
    skel = box // 2
    order_col = skeleton_order[0, 0].T
    vm = lambda *shape: pltpu.VMEM(shape, F32)
    widths = [w.shape[3] for w in weights[:4]]
    scratch = [
        vm(4, 5 * skel, rows), vm(4, box, rows), vm(4, 5 * skel, rows), vm(4, 4, skel, rows),
        vm(1, widths[1], rows), vm(3, widths[2], rows), vm(7, widths[3], rows),
        vm(1, box // 2, rows), vm(3, box // 4, rows), vm(7, box // 8, rows),
        vm(4, box, rows),
        vm(2, skel, widths[1]), vm(4, skel, widths[2]), vm(8, skel, widths[3]),
        vm(box, widths[0]), vm(box, widths[1]), vm(box, widths[2]), vm(box, widths[3]),
        vm(box, rows), vm(4, skel, rows), vm(skel, rows), vm(4, skel, rows),
        pltpu.VMEM((box, box), BF16),
        pltpu.SemaphoreType.DMA((128,)), pltpu.SemaphoreType.DMA((128,)),
    ]
    return pl.pallas_call(
        functools.partial(kernel, size_x, size_y),
        out_shape=jax.ShapeDtypeStruct(right_sides.shape, F32),
        in_specs=[pl.BlockSpec(memory_space=pltpu.VMEM)] * (3 + len(weights)),
        out_specs=pl.BlockSpec(memory_space=pltpu.VMEM),
        scratch_shapes=scratch,
        compiler_params=pltpu.CompilerParams(
            collective_id=0, has_side_effects=True, vmem_limit_bytes=60 * 2**20
        ),
    )(right_sides, order_col, skeleton_order, *weights)


def solution(mesh):
    four = P("bx", "by", None, None)
    five = P("bx", "by", None, None, None)
    in_specs = (four,) * 10 + (five,) * 4 + (four,)
    return jax.shard_map(
        functools.partial(body, mesh.shape["bx"], mesh.shape["by"]),
        mesh=mesh, in_specs=in_specs, out_specs=four, check_vma=False,
    )
```

profile of v0, /device:TPU:1, one launch (start us, length us, event | category | flops | bytes accessed | tf_op | source)
XLA Modules:
  0.0 208.7 jit_solution(12694037128971414410)
XLA Ops:
  0.0 0.0 copy-start.4
  0.0 0.0 copy-start.1
  0.0 0.0 copy-start.3
  0.0 1.8 copy.18.refs_5_
  1.8 1.7 copy.19.refs_6_
  3.5 1.7 copy.21.refs_9_
  5.2 0.0 copy-start.2
  5.2 1.8 copy.22.refs_10_
  7.0 1.7 copy.26.refs_15_
  8.7 1.9 copy.17.refs_4_
  10.6 0.0 copy-done.3
  10.6 0.0 copy-start
  10.6 0.9 copy.20.refs_8_
  11.5 0.0 copy-done.4
  11.5 0.9 copy.16
  12.4 0.0 copy-done.1
  12.4 1.3 copy.24.refs_13_
  13.7 0.0 copy-done.2
  13.7 1.3 copy.25.refs_14_
  15.0 0.0 copy-done
  15.0 1.8 copy.23.refs_12_
  16.8 190.1 %shard_map.145 = f32[1,1,128,768]{3,2,1,0:T(8,128)} custom-call(f32[1,1,128,768]{3,2,1,0:T(8,128)} %refs_0_.1, s32[768,4]{1,0:T(8,128)} %bitcast.3, s32[1,1,4,768]{3,2,1,0:T(4,128)} %refs_2_.1, f32[1,1,384,384]{3,2,1,0:T(8,128)} %refs_3_.1, f32[1,1,384,192]{3,2,1,0:T(8,128)} %copy.17.refs_4_, f32[1,1,384,96]{3,2,1,0:T(8,128)} %copy.18.refs_5_, ...), custom_call_target="tpu_custom_call" | custom-call | tf_op jit(solution)/shard_map/pallas_call | solution.py:334
  206.9 1.8 copy.28
Async XLA Ops:
  0.0 11.5 %copy-start.4 = (s32[1,1,4,768]{3,2,1,0:T(4,128)S(1)}, s32[1,1,4,768]{3,2,1,0:T(4,128)}, u32[]{:S(2)}) copy-start(s32[1,1,4,768]{3,2,1,0:T(4,128)} %refs_2_.1) | copy-start | bytes 36868
  0.0 12.4 %copy-start.1 = (f32[1,1,5,384,96]{3,4,2,1,0:T(8,128)S(1)}, f32[1,1,5,384,96]{3,4,2,1,0:T(8,128)}, u32[]{:S(2)}) copy-start(f32[1,1,5,384,96]{3,4,2,1,0:T(8,128)} %param.27) | copy-start | bytes 2211844
  0.0 10.5 %copy-start.3 = (f32[1,1,384,192]{2,3,1,0:T(8,128)S(1)}, f32[1,1,384,192]{2,3,1,0:T(8,128)}, u32[]{:S(2)}) copy-start(f32[1,1,384,192]{2,3,1,0:T(8,128)} %param.22) | copy-start | bytes 884740
  5.2 8.5 %copy-start.2 = (f32[1,1,5,384,48]{3,4,2,1,0:T(8,128)S(1)}, f32[1,1,5,384,48]{3,4,2,1,0:T(8,128)}, u32[]{:S(2)}) copy-start(f32[1,1,5,384,48]{3,4,2,1,0:T(8,128)} %param.28) | copy-start | bytes 1105924
  10.6 4.5 %copy-start = (f32[1,1,5,384,192]{3,4,2,1,0:T(8,128)S(1)}, f32[1,1,5,384,192]{3,4,2,1,0:T(8,128)}, u32[]{:S(2)}) copy-start(f32[1,1,5,384,192]{3,4,2,1,0:T(8,128)} %param.26) | copy-start | bytes 4423684
where the time goes:
time: 210 us; the launch traced here: 209 us
  Pallas kernels  190 us (90%)
  local copies, waits for them, and re-layouts  18.6 us (9%)
    pallas_call x1, Pallas kernels, body(): pl.pallas_call(functools.partial(kernel, size_x, size_y), out_shape=jax.S...  190 us
    unnamed x22, local copies, waits for them, and re-layouts  18.6 us

commit v1 on v0

--- a/solution.py
+++ b/solution.py
@@ -36,14 +36,22 @@
     return product(onehot, bh, dims) + product(onehot, bl, dims)
 
 
+class Reg:
+    def __init__(self): self.c=None
+    def __call__(self,name):
+        if self.c: self.c.__exit__(None,None,None)
+        self.c=jax.named_scope(name) if name else None
+        if self.c: self.c.__enter__()
+
+
 def flips(m):
     return (m >> 1) & 1, (m & 1) | ((m >> 2 & 1) << 1)
 
 
 def kernel(size_x, size_y, *refs):
-    (rhs, order_col, order_row, t0, t1, t2, t3, g0, g1, g2, g3, k0, k1, k2, k3, root, out) = refs[:17]
+    (rhs, order_row, t0, t1, t2, t3, g0, g1, g2, g3, k0, k1, k2, k3, root, out) = refs[:16]
     (ybuf, vbuf, qsend, qrecv, urecv1, urecv2, urecv3, xrecv1, xrecv2, xrecv3, xpart, tg1, tg2, tg3,
-     n0, n1, n2, n3, abuf, ypart, tpart, ssend, ptbuf, send, recv) = refs[17:]
+     n0, n1, n2, n3, abuf, ypart, tpart, ssend, ptbuf, order_col, send, recv) = refs[16:]
     interps, inverses, couples = (t0, t1, t2, t3), (g0, g1, g2, g3), (k0, k1, k2, k3)
     urecvs = (None, urecv1, urecv2, urecv3)
     xrecvs = (None, xrecv1, xrecv2, xrecv3)
@@ -95,6 +103,11 @@
     def rcopy(src, dst, s, dev):
         return pltpu.make_async_remote_copy(src, dst, send.at[s], recv.at[s], device_id=dev, device_id_type=MESH)
 
+    reg = Reg()
+    reg('zero')
+    order_f = order_row[0, 0].astype(F32)
+    order_f = jnp.concatenate([order_f, jnp.zeros((8 - order_f.shape[0], box), F32)], axis=0)
+    order_col[...] = order_f.T.astype(jnp.int32)
     for level in range(4):
         for k in (1, 2, 3, 4):
             there, _ = neighbour(level, k)
@@ -104,6 +117,7 @@
                 ybuf[level, pl.ds(k * skel, skel), :] = jnp.zeros((skel, ybuf.shape[2]), F32)
                 qrecv[level, k - 1] = jnp.zeros((skel, ybuf.shape[2]), F32)
 
+    reg('barrier')
     barrier = pltpu.get_barrier_semaphore()
     for m in range(1, 8):
         pl.semaphore_signal(barrier, 1, device_id=member(m), device_id_type=MESH)
@@ -123,6 +137,7 @@
             total = total + there.astype(jnp.int32)
     pl.semaphore_wait(barrier, total)
 
+    reg('sendint1')
     pending = []
 
     t_copies = [[], [], [], []]
@@ -138,28 +153,26 @@
 
     def make_n(level):
         own = inverses[level][0, 0]
-        cols = own.shape[1]
         if level == 0:
-            acc = dot3(interps[0][0, 0], own, NN)
-        else:
-            tgs[level][ranks[level]] = interps[level][0, 0]
-            for c in t_copies[level]:
-                c.wait_recv()
-            shared = []
-            for m in [m for m in range(1 << level) if not m & 2 and level > 1]:
-                block = rank_of(level, m)
-                held = interps[level].at[0, 0] if m == 0 else tgs[level].at[block]
-                c = rcopy(held, tgs[level].at[block], slot(), member(2))
-                c.start()
-                shared.append(c)
-                pending.append(c)
-            for c in shared:
-                c.wait_recv()
-            acc = jnp.zeros((skel, cols), F32)
-            for q in range(1 << level):
-                acc = acc + dot3(tgs[level][q], inverses[level][0, 0, q * cols:(q + 1) * cols, :], NN)
-        ns[level][:skel, :] = -acc
-        ns[level][skel:, :] = own
+            ns[0][:skel, :] = -dot3(interps[0][0, 0], own, NN)
+            ns[0][skel:, :] = own
+            return
+        cols = own.shape[0]
+        tgs[level][ranks[level]] = interps[level][0, 0]
+        for c in t_copies[level]:
+            c.wait_recv()
+        shared = []
+        for m in [m for m in range(1 << level) if not m & 2 and level > 1]:
+            block = rank_of(level, m)
+            held = interps[level].at[0, 0] if m == 0 else tgs[level].at[block]
+            c = rcopy(held, tgs[level].at[block], slot(), member(2))
+            c.start()
+            shared.append(c)
+            pending.append(c)
+        for c in shared:
+            c.wait_recv()
+        ns[level][:, :skel] = -dot3(own, tgs[level][...].reshape(skel, skel), NN)
+        ns[level][:, skel:] = own
 
     def onehot_pt(level):
         lanes = lax.broadcasted_iota(jnp.int32, (box, box), 1)
@@ -170,7 +183,8 @@
         return jnp.where(rows == order_row[0, 0, level:level + 1, :], 1.0, 0.0).astype(BF16)
 
     for level in range(4):
-        cols = interps[level].shape[3]
+        reg(f'f{level}_a')
+        cols = skel >> level
         rank = ranks[level]
         rows = pl.ds(pl.multiple_of(rank * cols, cols), cols)
         if level == 0:
@@ -178,7 +192,8 @@
             abuf[...] = pick_left(onehot_pt(0), rhs[0, 0], NT)
         else:
             abuf[...] = pick_left(ptbuf[...], vbuf[level - 1], NN)
-        y_own = dot3(ns[level][...], abuf[...], TN)
+        reg(f'f{level}_y')
+        y_own = dot3(ns[level][...], abuf[...], NN if level else TN)
         ypart[level, :cols, :] = y_own
         ybuf[level, rows, :] = y_own
         gathers = []
@@ -187,8 +202,10 @@
             c.start()
             gathers.append(c)
             pending.append(c)
+        reg(f'f{level}_ygwait')
         for c in gathers:
             c.wait_recv()
+        reg(f'f{level}_nbsend')
         for k in level_has[level]:
             s = slot()
             far = opposite[k]
@@ -202,9 +219,11 @@
         base = count[0] - len(level_has[level])
         if level < 2:
             send_interp(level + 2)
+        reg(f'f{level}_make')
         if level < 3:
             make_n(level + 1)
             ptbuf[...] = onehot_pt(level + 1)
+        reg(f'f{level}_nbwait')
         for k in level_has[level]:
             there, dev = neighbour(level, k)
             sent_as = level_has[level].index(opposite[k])
@@ -213,8 +232,13 @@
             @pl.when(there)
             def _():
                 c.wait_recv()
-        coupling = couples[level][0, 0].reshape(5 * skel, cols)
-        s_own = abuf[rows, :] - dot3(coupling, ybuf[level], TN)
+        reg(f'f{level}_s')
+        if level == 0:
+            s_own = abuf[...][:skel] - dot3(couples[0][0, 0].reshape(5 * skel, skel), ybuf[0], TN)
+        else:
+            s_own = abuf[rows, :]
+            for k in range(5):
+                s_own = s_own - dot3(couples[level][0, 0, k], ybuf[level, k * skel:(k + 1) * skel, :], NN)
         ssend[level, :cols, :] = s_own
         wide = min(level + 1, 3)
         spot = pl.ds(pl.multiple_of(ranks[wide] * cols, cols), cols)
@@ -225,19 +249,25 @@
             c.start()
             gathers.append(c)
             pending.append(c)
+        reg(f'f{level}_sgwait')
         for c in gathers:
             c.wait_recv()
 
-    t_own = dot3(root[0, 0], vbuf[3, :skel, :], TN)
+    reg('root')
+    t_own = dot3(root[0, 0], vbuf[3, :skel, :], NN)
 
     for level in (3, 2, 1, 0):
-        cols = interps[level].shape[3]
+        cols = skel >> level
         rank = ranks[level]
         members = 1 << level
         rows = pl.ds(pl.multiple_of(rank * cols, cols), cols)
+        reg(f'b{level}_q')
         tpart[:cols, :] = t_own
-        q = dot3(couples[level][0, 0].reshape(5 * skel, cols), t_own, NN)
-        qsend[level] = q
+        if level == 0:
+            qsend[0] = dot3(couples[0][0, 0].reshape(5 * skel, cols), t_own, NN)
+        else:
+            for k in range(5):
+                qsend[level, k * skel:(k + 1) * skel, :] = dot3(couples[level][0, 0, k], t_own, TN)
         base = count[0]
         for k in level_has[level]:
             s = slot()
@@ -248,13 +278,15 @@
             def _():
                 c.start()
             pending.append((there, c))
+        reg(f'b{level}_t')
         y_own = ypart[level, :cols, :]
-        abuf[:skel, :] = -dot3(interps[level][0, 0], y_own, NN)
+        abuf[:skel, :] = -dot3(interps[level][0, 0], y_own, TN if level else NN)
         abuf[skel:, :] = jnp.zeros_like(abuf[skel:, :])
         abuf[rows, :] = abuf[rows, :] + t_own
         rows_y = pl.ds(pl.multiple_of(skel + rank * cols, 8), cols)
         abuf[rows_y, :] = y_own
         ptbuf[...] = onehot_p(level) if level > 0 else onehot_pt(0)
+        reg(f'b{level}_nbwait')
         for k in level_has[level]:
             there, dev = neighbour(level, k)
             sent_as = level_has[level].index(opposite[k])
@@ -263,7 +295,8 @@
             @pl.when(there)
             def _():
                 c.wait_recv()
-        u = q[:skel] + ((qrecv[level, 0] + qrecv[level, 1]) + (qrecv[level, 2] + qrecv[level, 3]))
+        reg(f'b{level}_u')
+        u = qsend[level, :skel, :] + ((qrecv[level, 0] + qrecv[level, 1]) + (qrecv[level, 2] + qrecv[level, 3]))
         if level > 0:
             qsend[level, :skel, :] = u
             gathers = []
@@ -273,15 +306,19 @@
                 c.start()
                 gathers.append(c)
                 pending.append(c)
+            reg(f'b{level}_uwait')
             for c in gathers:
                 c.wait_recv()
+            reg(f'b{level}_u2')
             u_own = qsend[level, rows, :]
             for m in range(1, members):
                 u_own = u_own + urecvs[level][m - 1]
         else:
             u_own = u
-        comb = -dot3(ns[level][...], u_own, NN)
+        reg(f'b{level}_comb')
+        comb = -dot3(ns[level][...], u_own, TN if level else NN)
         abuf[...] = abuf[...] + comb
+        reg(f'b{level}_x')
         if level > 0:
             xpart[level] = pick_left(ptbuf[...], abuf[...], NN)
             size = box // members
@@ -292,8 +329,10 @@
                 c.start()
                 gathers.append(c)
                 pending.append(c)
+            reg(f'b{level}_xwait')
             for c in gathers:
                 c.wait_recv()
+            reg(f'b{level}_x2')
             t_own = xpart[level, pl.ds(pl.multiple_of(rank * size, size), size), :]
             for m in range(1, members):
                 t_own = t_own + xrecvs[level][m - 1]
@@ -302,6 +341,7 @@
             pt = ptbuf[...]
             out[0, 0] = product(ch, pt, TN) + product(cl, pt, TN)
 
+    reg('drain')
     for item in pending:
         if isinstance(item, tuple):
             there, c = item
@@ -311,36 +351,37 @@
                 c.wait_send()
         else:
             item.wait_send()
+    reg(None)
 
 
 def body(size_x, size_y, right_sides, skeleton_order, *weights):
     rows = right_sides.shape[2]
     box = right_sides.shape[3]
     skel = box // 2
-    order_col = skeleton_order[0, 0].T
+    weights = [jnp.swapaxes(w, -1, -2) if w.shape[-1] < skel else w for w in weights]
     vm = lambda *shape: pltpu.VMEM(shape, F32)
-    widths = [w.shape[3] for w in weights[:4]]
+    widths = [skel >> level for level in range(4)]
     scratch = [
         vm(4, 5 * skel, rows), vm(4, box, rows), vm(4, 5 * skel, rows), vm(4, 4, skel, rows),
         vm(1, widths[1], rows), vm(3, widths[2], rows), vm(7, widths[3], rows),
         vm(1, box // 2, rows), vm(3, box // 4, rows), vm(7, box // 8, rows),
         vm(4, box, rows),
-        vm(2, skel, widths[1]), vm(4, skel, widths[2]), vm(8, skel, widths[3]),
-        vm(box, widths[0]), vm(box, widths[1]), vm(box, widths[2]), vm(box, widths[3]),
+        vm(2, widths[1], skel), vm(4, widths[2], skel), vm(8, widths[3], skel),
+        vm(box, widths[0]), vm(widths[1], box), vm(widths[2], box), vm(widths[3], box),
         vm(box, rows), vm(4, skel, rows), vm(skel, rows), vm(4, skel, rows),
-        pltpu.VMEM((box, box), BF16),
+        pltpu.VMEM((box, box), BF16), pltpu.VMEM((box, 8), jnp.int32),
         pltpu.SemaphoreType.DMA((128,)), pltpu.SemaphoreType.DMA((128,)),
     ]
     return pl.pallas_call(
         functools.partial(kernel, size_x, size_y),
         out_shape=jax.ShapeDtypeStruct(right_sides.shape, F32),
-        in_specs=[pl.BlockSpec(memory_space=pltpu.VMEM)] * (3 + len(weights)),
+        in_specs=[pl.BlockSpec(memory_space=pltpu.VMEM)] * (2 + len(weights)),
         out_specs=pl.BlockSpec(memory_space=pltpu.VMEM),
         scratch_shapes=scratch,
         compiler_params=pltpu.CompilerParams(
             collective_id=0, has_side_effects=True, vmem_limit_bytes=60 * 2**20
         ),
-    )(right_sides, order_col, skeleton_order, *weights)
+    )(right_sides, skeleton_order, *weights)
 
 
 def solution(mesh):

time: 210 us -> 183 us (0.87)
  local copies, waits for them, and re-layouts: 18.6 us -> 1.77 us
  Pallas kernels: 190 us -> 179 us
    unnamed x22 -> x1, local copies, waits for them, and re-layouts: 18.6 us -> 1.77 us
    pallas_call x1, Pallas kernels: 190 us -> 179 us  [body(): pl.pallas_call(functools.partial(kernel, size_x, size_y), out_shape=jax.S...]
where the time goes in v1:
time: 183 us; the launch traced here: 181 us
  Pallas kernels  179 us (98%)
    pallas_call x1, Pallas kernels, body(): pl.pallas_call(functools.partial(kernel, size_x, size_y), out_shape=jax.S...  179 us

profile of v1, /device:TPU:1, one launch (start us, length us, event | category | flops | bytes accessed | tf_op | source)
XLA Modules:
  0.0 180.8 jit_solution(3160753863062662806)
XLA Ops:
  0.0 179.0 %shard_map.145 = f32[1,1,128,768]{3,2,1,0:T(8,128)} custom-call(f32[1,1,128,768]{3,2,1,0:T(8,128)} %refs_0_.1, s32[1,1,4,768]{3,2,1,0:T(4,128)} %refs_1_.1, f32[1,1,384,384]{3,2,1,0:T(8,128)} %refs_2_.1, f32[1,1,192,384]{3,2,1,0:T(8,128)} %bitcast.13, f32[1,1,96,384]{3,2,1,0:T(8,128)} %bitcast.15, f32[1,1,48,384]{3,2,1,0:T(8,128)} %bitcast.17, ...), custom_call_target="tpu_custom_call" | custom-call | tf_op jit(solution)/shard_map/pallas_call | solution.py:375
  179.1 1.8 copy.17

commit v2 on v0

v2 whole, which is shorter than its diff:
```python
import functools

import jax
import jax.numpy as jnp
from jax import lax
from jax.experimental import pallas as pl
from jax.experimental.pallas import tpu as pltpu
from jax.sharding import PartitionSpec as P

REACH = ((1, 1), (1, 2), (2, 2), (2, 4))
OPPOSITE = {1: 2, 2: 1, 3: 4, 4: 3}
F32 = jnp.float32
BF16 = jnp.bfloat16
MESH = pl.DeviceIdType.MESH
NN = (((1,), (0,)), ((), ()))
TN = (((0,), (0,)), ((), ()))
NT = (((1,), (1,)), ((), ()))


def halves(x):
    high = x.astype(BF16)
    return high, (x - high.astype(F32)).astype(BF16)


def product(a, b, dims):
    return lax.dot_general(a, b, dims, preferred_element_type=F32)


def dot3(a, b, dims):
    ah, al = halves(a)
    bh, bl = halves(b)
    return product(ah, bh, dims) + (product(ah, bl, dims) + product(al, bh, dims))


def pick_left(onehot, b, dims):
    bh, bl = halves(b)
    return product(onehot, bh, dims) + product(onehot, bl, dims)


def pick_right(a, onehot, dims):
    ah, al = halves(a)
    return product(ah, onehot, dims) + product(al, onehot, dims)


class Phases:
    def __init__(self):
        self.scope = None

    def __call__(self, name):
        if self.scope:
            self.scope.__exit__(None, None, None)
        self.scope = jax.named_scope(name) if name else None
        if self.scope:
            self.scope.__enter__()


def kernel(size_x, size_y, *refs):
    (rhs_in, order_in, t0_in, t1_in, t2_in, t3_in, g0_in, g1_in, g2_in, g3_in,
     k0_in, k1_in, k2_in, k3_in, root_in, out) = refs[:16]
    (rhs, order_row, t0, tg1, tg2, g0, g1, g2, k0, k1, k2,
     ybuf, vbuf, qsend, qrecv, urecv1, urecv2, xrecv1, xrecv2, xpart,
     n0, n1, n2, abuf, ypart, ssend, ptbuf, order_col,
     top, turned, v3, y3, yr3, q3, qr3, x3, back3, pick3, local, send, recv) = refs[16:]
    inverses, couples = (g0, g1, g2), (k0, k1, k2)
    urecvs, xrecvs, tgs, ns = (None, urecv1, urecv2), (None, xrecv1, xrecv2), (None, tg1, tg2), (n0, n1, n2)
    skel = t0.shape[0]
    box = 2 * skel
    rhs_count = ybuf.shape[2]
    share = v3.shape[1]
    kinds = top.shape[0] - 3
    phase = Phases()
    i, j = lax.axis_index("bx"), lax.axis_index("by")
    bits = (lax.rem(j, 2), lax.rem(i, 2), lax.rem(lax.div(j, 2), 2))
    inner = bits[0] != bits[2]
    outer = jnp.logical_not(inner)

    def flipped(b, m):
        return (1 - bits[b]) if m >> b & 1 else bits[b]

    def member(m):
        return (i + (flipped(1, m) - bits[1]), j + (flipped(0, m) - bits[0]) + 2 * (flipped(2, m) - bits[2]))

    def rank_of(level, m):
        rank = jnp.int32(0)
        for b in range(level):
            rank = rank + (1 << b) * flipped(b, m)
        return rank

    def part_of(m):
        return flipped(1, m) + 2 * flipped(2, m)

    def span(start, size):
        return pl.ds(pl.multiple_of(start * size, size), size)

    def neighbour(level, k):
        rx, ry = REACH[level]
        if k == 1:
            return i >= rx, (i - rx, j)
        if k == 2:
            return i + rx < size_x, (i + rx, j)
        if k == 3:
            return j >= ry, (i, j - ry)
        return j + ry < size_y, (i, j + ry)

    has = [[k for k in (1, 2, 3, 4) if (REACH[l][0] < size_x if k < 3 else REACH[l][1] < size_y)] for l in range(4)]
    cross = [[k for k in has[l] if k < 3] for l in range(4)]
    along = [[k for k in has[l] if k > 2] for l in range(4)]

    count = [0]
    pending = []

    def slot():
        count[0] += 1
        return count[0] - 1

    def rcopy(src, dst, s, dev):
        return pltpu.make_async_remote_copy(src, dst, send.at[s], recv.at[s], device_id=dev, device_id_type=MESH)

    def go(c, when=None):
        pending.append((when, c))
        if when is None:
            c.start()
        else:
            @pl.when(when)
            def _():
                c.start()

    def come(c, when=None):
        if when is None:
            c.wait_recv()
        else:
            @pl.when(when)
            def _():
                c.wait_recv()

    phase("start")
    rank = [rank_of(l, 0) for l in range(4)]
    loads = {}

    def load(name, src, dst):
        c = pltpu.make_async_copy(src, dst, local.at[len(loads)])
        loads[name] = c
        c.start()

    def need(*names):
        for name in names:
            loads[name].wait()

    load("order", order_in.at[0, 0], order_row)
    load("t0", t0_in.at[0, 0], t0)
    load("g0", g0_in.at[0, 0], g0)
    load("rhs", rhs_in.at[0, 0], rhs)
    load("t1", t1_in.at[0, 0], tg1.at[rank[1]])
    load("k0", k0_in.at[0, 0], k0)
    load("t2", t2_in.at[0, 0], tg2.at[rank[2]])
    load("g1", g1_in.at[0, 0], g1)
    load("t3", t3_in.at[0, 0], top.at[0, rank[3]])
    load("g3", g3_in.at[0, 0], top.at[1, rank[3]])
    load("root", root_in.at[0, 0], top.at[2, rank[3]])
    load("k3", k3_in.at[0, 0, pl.ds(0, kinds)], top.at[pl.ds(3, kinds), rank[3]])
    load("k1", k1_in.at[0, 0], k1)
    load("g2", g2_in.at[0, 0], g2)
    load("k2", k2_in.at[0, 0], k2)

    barrier = pltpu.get_barrier_semaphore()
    for m in range(1, 8):
        pl.semaphore_signal(barrier, 1, device_id=member(m), device_id_type=MESH)
    total = jnp.int32(7)
    greeted = set()
    for level in range(4):
        for k in has[level]:
            key = (k, REACH[level][0] if k < 3 else REACH[level][1])
            if key in greeted:
                continue
            greeted.add(key)
            there, dev = neighbour(level, k)

            @pl.when(there)
            def _():
                pl.semaphore_signal(barrier, 1, device_id=dev, device_id_type=MESH)
            total = total + there.astype(jnp.int32)

    for level in range(3):
        for k in (1, 2, 3, 4):
            there, _ = neighbour(level, k)

            @pl.when(jnp.logical_not(there))
            def _():
                ybuf[level, k * skel:(k + 1) * skel, :] = jnp.zeros((skel, rhs_count), F32)
                qrecv[level, k - 1] = jnp.zeros((skel, rhs_count), F32)
    for k in has[3]:
        there, _ = neighbour(3, k)

        @pl.when(jnp.logical_not(there))
        def _():
            yr3[k - 1] = jnp.zeros(yr3.shape[1:], F32)
            qr3[k - 1] = jnp.zeros(qr3.shape[1:], F32)
    turned[...] = jnp.zeros_like(turned)

    chunks = range((top.shape[0] + 1) // 2)
    slots_own, slots_in, slots_on = ([slot() for _ in chunks] for _ in range(3))
    slots_mate = [slot() for _ in range(4)]

    def chunk_copy(c, block, dev, s):
        at = pl.ds(2 * c, min(2, top.shape[0] - 2 * c))
        return rcopy(top.at[at, block], top.at[at, block], s, dev)

    def mate_copy(n, mine):
        block = rank_of(3, (0, 1, 5, 4)[n] ^ (0 if mine else 2))
        return rcopy(top.at[:, block], top.at[:, block], slots_mate[n], member(2))

    def outer_send(c):
        go(chunk_copy(c, rank[3], member(1), slots_own[c]), outer)

    def inner_send():
        for c in chunks:
            go(chunk_copy(c, rank[3], member(5), slots_in[c]), inner)

    def inner_forward(c):
        come(chunk_copy(c, rank_of(3, 1), member(1), slots_own[c]), inner)
        go(chunk_copy(c, rank_of(3, 1), member(5), slots_on[c]), inner)

    def mate_send(n):
        for c in chunks:
            if n == 2:
                come(chunk_copy(c, rank_of(3, 5), member(5), slots_in[c]), inner)
            if n == 3:
                come(chunk_copy(c, rank_of(3, 4), member(5), slots_on[c]), inner)
        go(mate_copy(n, True), inner)

    def onehot_pt(level):
        lanes = lax.broadcasted_iota(jnp.int32, (box, box), 1)
        return jnp.where(lanes == order_col[:, level:level + 1], 1.0, 0.0).astype(BF16)

    def onehot_p(level):
        rows = lax.broadcasted_iota(jnp.int32, (box, box), 0)
        return jnp.where(rows == order_row[level:level + 1, :], 1.0, 0.0).astype(BF16)

    def make_n(level):
        if level == 0:
            need("t0", "g0")
            n0[:skel, :] = -dot3(t0[...], g0[...], NN)
            n0[skel:, :] = g0[...]
            return
        need(f"g{level}")
        own = inverses[level][...]
        ns[level][:, :skel] = -dot3(own, tgs[level][...].reshape(skel, skel), NN)
        ns[level][:, skel:] = own

    need("order")
    order_f = order_row[...].astype(F32)
    order_f = jnp.concatenate([order_f, jnp.zeros((8 - order_f.shape[0], box), F32)], axis=0)
    order_col[...] = order_f.T.astype(jnp.int32)

    phase("f0_make")
    make_n(0)
    phase("f0_a")
    need("rhs")
    abuf[...] = pick_left(onehot_pt(0), rhs[...], NT)
    phase("f0_y")
    y_own = dot3(n0[...], abuf[...], TN)
    ybuf[0, :skel, :] = y_own
    ypart[0] = y_own
    phase("f0_barrier")
    pl.semaphore_wait(barrier, total)
    phase("f0_send")
    slots_y0 = {k: slot() for k in has[0]}
    for k in along[0] + cross[0]:
        there, dev = neighbour(0, k)
        far = OPPOSITE[k]
        go(rcopy(ypart.at[0], ybuf.at[0, pl.ds(far * skel, skel), :], slots_y0[k], dev), there)
    need("t1")
    t1_copy = rcopy(tg1.at[rank[1]], tg1.at[rank[1]], slot(), member(1))
    go(t1_copy)
    need("t3", "g3", "root", "k3")
    inner_send()
    mate_send(0)
    phase("f0_s")
    need("k0")
    s_own = abuf[:skel, :] - dot3(k0[0], ypart[0], TN)
    ptbuf[...] = onehot_pt(1)
    for k in cross[0] + along[0]:
        there, dev = neighbour(0, k)
        phase(f"f0_wait{k}")
        come(rcopy(ypart.at[0], ybuf.at[0, pl.ds(k * skel, skel), :], slots_y0[OPPOSITE[k]], dev), there)
        phase(f"f0_s{k}")
        s_own = s_own - dot3(k0[k], ybuf[0, k * skel:(k + 1) * skel, :], TN)
    ssend[0] = s_own
    vbuf[0, span(rank[1], skel), :] = s_own
    give = rcopy(ssend.at[0], vbuf.at[0, span(rank[1], skel), :], slot(), member(1))
    go(give)
    need("t2")
    t2_slots = [slot() for _ in range(3)]
    go(rcopy(tg2.at[rank[2]], tg2.at[rank[2]], t2_slots[0], member(1)))
    go(rcopy(tg2.at[rank[2]], tg2.at[rank[2]], t2_slots[1], member(2)))
    outer_send(0)
    phase("f0_n1")
    come(t1_copy)
    make_n(1)
    phase("f0_gwait")
    come(give)

    for level in (1, 2):
        phase(f"f{level}_a")
        cols = skel >> level
        mine = rank[level]
        rows = span(mine, cols)
        abuf[...] = pick_left(ptbuf[...], vbuf[level - 1], NN)
        phase(f"f{level}_y")
        y_own = dot3(ns[level][...], abuf[...], NN)
        ypart[level, :cols, :] = y_own
        ybuf[level, rows, :] = y_own

        def at(k, m):
            return ybuf.at[level, pl.ds(pl.multiple_of(k * skel + rank_of(level, m) * cols, cols), cols), :]

        def pair(k, m, to, s):
            return rcopy(at(k, m), at(k, m), s, member(to))

        own_src = ypart.at[level, pl.ds(0, cols), :]
        s_a = [slot() for _ in range(3)]
        s_c = {k: [slot(), slot()] for k in cross[level]}
        s_b = {k: slot() for k in along[level]}
        s_d = {k: [slot() for _ in range(3)] for k in along[level]}
        s_e = {k: [slot(), slot()] for k in cross[level]}
        phase(f"f{level}_send")
        go(rcopy(own_src, at(0, 0), s_a[0], member(1)))
        for k in along[level]:
            there, dev = neighbour(level, k)
            go(rcopy(own_src, at(OPPOSITE[k], 0), s_b[k], dev), there)
        if level == 2:
            go(rcopy(own_src, at(0, 0), s_a[1], member(2)))
        for k in cross[level]:
            there, dev = neighbour(level, k)
            go(rcopy(own_src, at(OPPOSITE[k], 0), s_c[k][0], dev), there)
        if level == 1:
            ptbuf[...] = onehot_pt(2)
        phase(f"f{level}_ywait")
        come(pair(0, 1, 1, s_a[0]))
        if level == 2:
            go(pair(0, 1, 2, s_a[2]))
        for k in cross[level]:
            there, dev = neighbour(level, k)
            go(rcopy(at(0, 1), at(OPPOSITE[k], 1), s_c[k][1], dev), there)
        if level == 1:
            outer_send(1)
            inner_forward(0)
        else:
            come(pair(0, 2, 2, s_a[1]))
            come(pair(0, 3, 2, s_a[2]))
            inner_forward(2)
        phase(f"f{level}_s0")
        need(f"k{level}")
        s_own = abuf[rows, :] - dot3(couples[level][0], ybuf[level, :skel, :], NN)
        phase(f"f{level}_relay")
        for k in cross[level]:
            there, dev = neighbour(level, k)
            come(rcopy(own_src, at(k, 0), s_c[OPPOSITE[k]][0], dev), there)
            if level == 2:
                go(pair(k, 0, 2, s_e[k][0]), there)
        for k in along[level]:
            there, dev = neighbour(level, k)
            come(rcopy(own_src, at(k, 0), s_b[OPPOSITE[k]], dev), there)
            go(pair(k, 0, 1, s_d[k][0]), there)
            if level == 2:
                go(pair(k, 0, 2, s_d[k][1]), there)
        for k in cross[level]:
            there, dev = neighbour(level, k)
            come(rcopy(own_src, at(k, 1), s_c[OPPOSITE[k]][1], dev), there)
            if level == 2:
                go(pair(k, 1, 2, s_e[k][1]), there)
        if level == 2:
            phase("f2_pick3")

            @pl.when(inner)
            def _():
                o = order_row[3:4, :]
                block = turned.shape[1]
                o = o + sum((block - cols) * (o >= cols * b).astype(jnp.int32) for b in range(1, 8))
                lines = lax.broadcasted_iota(jnp.int32, pick3.shape, 0)
                pick3[...] = jnp.where(lines == o, 1.0, 0.0).astype(BF16)
            mate_send(1)
            mate_send(2)
        for k in cross[level]:
            there, dev = neighbour(level, k)
            phase(f"f{level}_cross{k}")
            if level == 2:
                come(pair(k, 2, 2, s_e[k][0]), there)
                come(pair(k, 3, 2, s_e[k][1]), there)
            s_own = s_own - dot3(couples[level][k], ybuf[level, k * skel:(k + 1) * skel, :], NN)
        for k in along[level]:
            there, dev = neighbour(level, k)
            phase(f"f{level}_along{k}")
            come(pair(k, 1, 1, s_d[k][0]), there)
            if level == 2:
                go(pair(k, 1, 2, s_d[k][2]), there)
                come(pair(k, 2, 2, s_d[k][1]), there)
                come(pair(k, 3, 2, s_d[k][2]), there)
            s_own = s_own - dot3(couples[level][k], ybuf[level, k * skel:(k + 1) * skel, :], NN)
        if level == 2:
            turned[:, :cols] = s_own.T
            continue
        phase("f1_gsend")
        ssend[1, :cols, :] = s_own
        at_v = lambda m: vbuf.at[1, span(rank_of(2, m), cols), :]
        vbuf[1, span(rank[2], cols), :] = s_own
        s_g = [slot() for _ in range(3)]
        go(rcopy(ssend.at[1, pl.ds(0, cols), :], at_v(0), s_g[0], member(1)))
        go(rcopy(ssend.at[1, pl.ds(0, cols), :], at_v(0), s_g[1], member(2)))
        outer_send(2)
        come(rcopy(tg2.at[rank_of(2, 1)], tg2.at[rank_of(2, 1)], t2_slots[0], member(1)))
        go(rcopy(tg2.at[rank_of(2, 1)], tg2.at[rank_of(2, 1)], t2_slots[2], member(2)))
        come(rcopy(tg2.at[rank_of(2, 2)], tg2.at[rank_of(2, 2)], t2_slots[1], member(2)))
        come(rcopy(tg2.at[rank_of(2, 3)], tg2.at[rank_of(2, 3)], t2_slots[2], member(2)))
        phase("f1_n2")
        make_n(2)
        phase("f1_gwait")
        come(rcopy(at_v(1), at_v(1), s_g[0], member(1)))
        go(rcopy(at_v(1), at_v(1), s_g[2], member(2)))
        inner_forward(1)
        come(rcopy(at_v(2), at_v(2), s_g[1], member(2)))
        come(rcopy(at_v(3), at_v(3), s_g[2], member(2)))

    phase("l3_send")
    own_part = span(part_of(0), share)
    s_t = [slot() for _ in range(8)]
    s_x = [slot() for _ in range(8)]
    s_y3 = {k: slot() for k in has[3]}
    s_q3 = {k: slot() for k in has[3]}
    aside = lambda m: (m & 1) ^ (m >> 2 & 1)
    for m in range(1, 8):
        go(rcopy(turned.at[span(part_of(m), share)], v3.at[rank[3]], s_t[m], member(m)), outer if aside(m) else inner)
    mate_send(3)
    for n in range(4):
        come(mate_copy(n, False), inner)

    @pl.when(inner)
    def _():
        phase("l3_in")
        v3[rank[3]] = turned[own_part, :]
        for m in range(1, 8):
            come(rcopy(turned.at[own_part], v3.at[rank_of(3, m)], s_t[m], member(m)))
        full = lambda n: top[n].reshape(skel, skel)
        phase("l3_y")
        a = pick_right(jnp.concatenate([v3[b] for b in range(8)], axis=1), pick3[...], NN)
        s0, r0 = a[:, :skel], a[:, skel:]
        y = dot3(r0 - dot3(s0, full(0), NT), full(1), NT)
        y3[...] = y
        for k in has[3]:
            there, dev = neighbour(3, k)

            @pl.when(there)
            def _():
                rcopy(y3, yr3.at[OPPOSITE[k] - 1], s_y3[k], dev).start()
        phase("l3_s")
        s = s0 - dot3(y, full(3), NT)
        for k in has[3]:
            there, dev = neighbour(3, k)
            come(rcopy(y3, yr3.at[k - 1], s_y3[OPPOSITE[k]], dev), there)
            s = s - dot3(yr3[k - 1], full(3 + k), NT)
        phase("l3_q")
        t = dot3(s, full(2), NT)
        for k in has[3]:
            q3[k - 1] = dot3(t, full(3 + k), NN)
            there, dev = neighbour(3, k)

            @pl.when(there)
            def _():
                rcopy(q3.at[k - 1], qr3.at[OPPOSITE[k] - 1], s_q3[k], dev).start()
        u = dot3(t, full(3), NN)
        phase("l3_u")
        for k in has[3]:
            there, dev = neighbour(3, k)
            come(rcopy(q3.at[k - 1], qr3.at[k - 1], s_q3[OPPOSITE[k]], dev), there)
            u = u + qr3[k - 1]
        phase("l3_x")
        xr = y - dot3(u, full(1), NN)
        xs = t - dot3(xr, full(0), NN)
        xv = pick_right(jnp.concatenate([xs, xr], axis=1), pick3[...], NT)
        wide = turned.shape[1]
        for b in range(8):
            x3[b] = xv[:, b * wide:(b + 1) * wide]
        for m in range(1, 8):
            rcopy(x3.at[rank_of(3, m)], back3.at[own_part], s_x[m], member(m)).start()
        back3[own_part, :] = x3[rank[3]]
        phase(None)

    phase("l3_out")
    for m in range(1, 8):
        come(rcopy(x3.at[rank[3]], back3.at[span(part_of(m), share)], s_x[m], member(m)), outer if aside(m) else inner)
    t_own = back3[...].T[:skel >> 2]

    for level in (2, 1, 0):
        phase(f"b{level}_q")
        cols = skel >> level
        members = 1 << level
        rows = span(rank[level], cols)
        if level == 0:
            qsend[0] = dot3(k0[...].reshape(5 * skel, skel), t_own, NN)
        else:
            for k in range(5):
                qsend[level, k * skel:(k + 1) * skel, :] = dot3(couples[level][k], t_own, TN)
        s_q = {k: slot() for k in has[level]}
        for k in has[level]:
            there, dev = neighbour(level, k)
            go(rcopy(qsend.at[level, pl.ds(k * skel, skel), :], qrecv.at[level, OPPOSITE[k] - 1], s_q[k], dev), there)
        phase(f"b{level}_t")
        y_own = ypart[level, :cols, :]
        if level == 0:
            abuf[:skel, :] = t_own - dot3(t0[...], y_own, NN)
            abuf[skel:, :] = y_own
        else:
            abuf[:skel, :] = -dot3(tgs[level][rank[level]], y_own, TN)
            abuf[skel:, :] = jnp.zeros((skel, rhs_count), F32)
            abuf[rows, :] = abuf[rows, :] + t_own
            abuf[pl.ds(pl.multiple_of(skel + rank[level] * cols, 8), cols), :] = y_own
        ptbuf[...] = onehot_p(level) if level > 0 else onehot_pt(0)
        phase(f"b{level}_nbwait")
        for k in has[level]:
            there, dev = neighbour(level, k)
            come(rcopy(qsend.at[level, pl.ds(k * skel, skel), :], qrecv.at[level, k - 1], s_q[OPPOSITE[k]], dev), there)
        phase(f"b{level}_u")
        u = qsend[level, :skel, :] + ((qrecv[level, 0] + qrecv[level, 1]) + (qrecv[level, 2] + qrecv[level, 3]))
        if level > 0:
            qsend[level, :skel, :] = u
            gathers = []
            for m in range(1, members):
                c = rcopy(qsend.at[level, span(rank_of(level, m), cols), :], urecvs[level].at[m - 1], slot(), member(m))
                go(c)
                gathers.append(c)
            for c in gathers:
                come(c)
            u_own = qsend[level, rows, :]
            for m in range(1, members):
                u_own = u_own + urecvs[level][m - 1]
        else:
            u_own = u
        phase(f"b{level}_comb")
        abuf[...] = abuf[...] - dot3(ns[level][...], u_own, TN if level else NN)
        phase(f"b{level}_x")
        if level > 0:
            xpart[level] = pick_left(ptbuf[...], abuf[...], NN)
            size = box // members
            gathers = []
            for m in range(1, members):
                c = rcopy(xpart.at[level, span(rank_of(level, m), size), :], xrecvs[level].at[m - 1], slot(), member(m))
                go(c)
                gathers.append(c)
            phase(f"b{level}_xwait")
            for c in gathers:
                come(c)
            t_own = xpart[level, span(rank[level], size), :]
            for m in range(1, members):
                t_own = t_own + xrecvs[level][m - 1]
        else:
            ch, cl = halves(abuf[...])
            pt = ptbuf[...]
            out[0, 0] = product(ch, pt, TN) + product(cl, pt, TN)

    phase("drain")
    for when, c in pending:
        if when is None:
            c.wait_send()
        else:
            @pl.when(when)
            def _():
                c.wait_send()

    @pl.when(inner)
    def _():
        for k in has[3]:
            there, dev = neighbour(3, k)

            @pl.when(there)
            def _():
                rcopy(y3, yr3.at[OPPOSITE[k] - 1], s_y3[k], dev).wait_send()
                rcopy(q3.at[k - 1], qr3.at[OPPOSITE[k] - 1], s_q3[k], dev).wait_send()
        for m in range(1, 8):
            rcopy(x3.at[rank_of(3, m)], back3.at[own_part], s_x[m], member(m)).wait_send()
    phase(None)


def body(size_x, size_y, right_sides, skeleton_order, *weights):
    rows = right_sides.shape[2]
    box = right_sides.shape[3]
    skel = box // 2
    weights = [jnp.swapaxes(w, -1, -2) if w.shape[-1] < skel else w for w in weights]
    vm = lambda *shape: pltpu.VMEM(shape, F32)
    widths = [skel >> level for level in range(4)]
    share = rows // 4
    kinds = 5 if size_y > REACH[3][1] else 3
    lanes = -(-widths[2] // 128) * 128
    scratch = [
        vm(rows, box), pltpu.VMEM((4, box), jnp.int32), vm(skel, skel), vm(2, widths[1], skel), vm(4, widths[2], skel),
        vm(skel, skel), vm(widths[1], skel), vm(widths[2], skel),
        vm(5, skel, skel), vm(5, widths[1], skel), vm(5, widths[2], skel),
        vm(3, 5 * skel, rows), vm(2, box, rows), vm(3, 5 * skel, rows), vm(3, 4, skel, rows),
        vm(1, widths[1], rows), vm(3, widths[2], rows),
        vm(1, box // 2, rows), vm(3, box // 4, rows),
        vm(3, box, rows),
        vm(box, widths[0]), vm(widths[1], box), vm(widths[2], box),
        vm(box, rows), vm(3, skel, rows), vm(2, skel, rows),
        pltpu.VMEM((box, box), BF16), pltpu.VMEM((box, 8), jnp.int32),
        vm(3 + kinds, 8, widths[3], skel), vm(rows, lanes), vm(8, share, lanes),
        vm(share, skel), vm(kinds - 1, share, skel), vm(kinds - 1, share, skel), vm(kinds - 1, share, skel),
        vm(8, share, lanes), vm(rows, lanes), pltpu.VMEM((8 * lanes, box), BF16),
        pltpu.SemaphoreType.DMA((16,)),
        pltpu.SemaphoreType.DMA((160,)), pltpu.SemaphoreType.DMA((160,)),
    ]
    return pl.pallas_call(
        functools.partial(kernel, size_x, size_y),
        out_shape=jax.ShapeDtypeStruct(right_sides.shape, F32),
        in_specs=[pl.BlockSpec(memory_space=pl.ANY)] * (2 + len(weights)),
        out_specs=pl.BlockSpec(memory_space=pltpu.VMEM),
        scratch_shapes=scratch,
        compiler_params=pltpu.CompilerParams(
            collective_id=0, has_side_effects=True, vmem_limit_bytes=60 * 2**20
        ),
    )(right_sides, skeleton_order, *weights)


def solution(mesh):
    four = P("bx", "by", None, None)
    five = P("bx", "by", None, None, None)
    in_specs = (four,) * 10 + (five,) * 4 + (four,)
    return jax.shard_map(
        functools.partial(body, mesh.shape["bx"], mesh.shape["by"]),
        mesh=mesh, in_specs=in_specs, out_specs=four, check_vma=False,
    )
```

time: 210 us -> 133 us (0.63)
  Pallas kernels: 190 us -> 131 us
  local copies, waits for them, and re-layouts: 18.6 us -> 1.77 us
    pallas_call x1, Pallas kernels: 190 us -> 131 us  [body(): pl.pallas_call(functools.partial(kernel, size_x, size_y), out_shape=jax.S...]
    unnamed x22 -> x1, local copies, waits for them, and re-layouts: 18.6 us -> 1.77 us
where the time goes in v2:
time: 133 us
  Pallas kernels  131 us (98%)
  local copies, waits for them, and re-layouts  1.77 us (1%)
    pallas_call x1, Pallas kernels, body(): pl.pallas_call(functools.partial(kernel, size_x, size_y), out_shape=jax.S...  131 us

profile of v2, /device:TPU:1, one launch (start us, length us, event | category | flops | bytes accessed | tf_op | source)
XLA Modules:
  0.0 132.6 jit_solution(6160754986085284253)
XLA Ops:
  0.0 130.9 %shard_map.145 = f32[1,1,128,768]{3,2,1,0:T(8,128)} custom-call(f32[1,1,128,768]{3,2,1,0:T(8,128)} %refs_0_.1, s32[1,1,4,768]{3,2,1,0:T(4,128)} %refs_1_.1, f32[1,1,384,384]{3,2,1,0:T(8,128)} %refs_2_.1, f32[1,1,192,384]{3,2,1,0:T(8,128)} %bitcast.13, f32[1,1,96,384]{3,2,1,0:T(8,128)} %bitcast.15, f32[1,1,48,384]{3,2,1,0:T(8,128)} %bitcast.17, ...), custom_call_target="tpu_custom_call" | custom-call | tf_op jit(solution)/shard_map/pallas_call | solution.py:610
  130.9 1.8 %copy.17 = f32[1,1,128,768]{3,2,1,0:T(8,128)} copy(f32[1,1,128,768]{3,2,1,0:T(8,128)} %shard_map.145) | data formatting | bytes 786432

commit v3 on v2

v3 whole, which is shorter than its diff:
```python
import functools

import jax
import jax.numpy as jnp
from jax import lax
from jax.experimental import pallas as pl
from jax.experimental.pallas import tpu as pltpu
from jax.sharding import PartitionSpec as P

REACH = ((1, 1), (1, 2), (2, 2), (2, 4))
OPPOSITE = {1: 2, 2: 1, 3: 4, 4: 3}
F32 = jnp.float32
BF16 = jnp.bfloat16
MESH = pl.DeviceIdType.MESH
NN = (((1,), (0,)), ((), ()))
TN = (((0,), (0,)), ((), ()))
NT = (((1,), (1,)), ((), ()))


def halves(x):
    high = x.astype(BF16)
    return high, (x - high.astype(F32)).astype(BF16)


def product(a, b, dims):
    return lax.dot_general(a, b, dims, preferred_element_type=F32)


def dot3(a, b, dims):
    ah, al = halves(a)
    bh, bl = halves(b)
    return product(ah, bh, dims) + (product(ah, bl, dims) + product(al, bh, dims))


def pick_left(onehot, b, dims):
    bh, bl = halves(b)
    return product(onehot, bh, dims) + product(onehot, bl, dims)


def pick_right(a, onehot, dims):
    ah, al = halves(a)
    return product(ah, onehot, dims) + product(al, onehot, dims)


class Phases:
    def __init__(self):
        self.scope = None

    def __call__(self, name):
        if self.scope:
            self.scope.__exit__(None, None, None)
        self.scope = jax.named_scope(name) if name else None
        if self.scope:
            self.scope.__enter__()


def kernel(size_x, size_y, *refs):
    (rhs_in, order_in, t0_in, t1_in, t2_in, t3_in, g0_in, g1_in, g2_in, g3_in,
     k0_in, k1_in, k2_in, k3_in, root_in, out) = refs[:16]
    (rhs, order_row, t0, tg1, g0, g1, k0, k1,
     ybuf, vbuf, qsend, qrecv, urecv1, xrecv1, xpart, base0, base1,
     n0, n1, abuf, ypart, ssend, ptbuf, order_col,
     mid, turned, v2, y2, yr2, q2, qr2, x2, back2, pick2, turn2, t2,
     top, v3, y3, yr3, q3, qr3, x3, pick3, local, send, recv) = refs[16:]
    skel = t0.shape[0]
    box = 2 * skel
    rhs_count = ybuf.shape[2]
    half, share = v2.shape[1], v3.shape[1]
    kinds = top.shape[0] - 3
    phase = Phases()
    i, j = lax.axis_index("bx"), lax.axis_index("by")
    bits = (lax.rem(j, 2), lax.rem(i, 2), lax.rem(lax.div(j, 2), 2))
    inner = bits[0] != bits[2]
    outer = jnp.logical_not(inner)

    def flipped(b, m):
        return (1 - bits[b]) if m >> b & 1 else bits[b]

    def member(m):
        return (i + (flipped(1, m) - bits[1]), j + (flipped(0, m) - bits[0]) + 2 * (flipped(2, m) - bits[2]))

    def rank_of(level, m):
        rank = jnp.int32(0)
        for b in range(level):
            rank = rank + (1 << b) * flipped(b, m)
        return rank

    def span(start, size):
        return pl.ds(pl.multiple_of(start * size, size), size)

    def neighbour(level, k):
        rx, ry = REACH[level]
        if k == 1:
            return i >= rx, (i - rx, j)
        if k == 2:
            return i + rx < size_x, (i + rx, j)
        if k == 3:
            return j >= ry, (i, j - ry)
        return j + ry < size_y, (i, j + ry)

    has = [[k for k in (1, 2, 3, 4) if (REACH[l][0] < size_x if k < 3 else REACH[l][1] < size_y)] for l in range(4)]
    cross = [[k for k in has[l] if k < 3] for l in range(4)]
    along = [[k for k in has[l] if k > 2] for l in range(4)]

    count = [0]
    pending = []

    def slot():
        count[0] += 1
        return count[0] - 1

    def rcopy(src, dst, s, dev):
        return pltpu.make_async_remote_copy(src, dst, send.at[s], recv.at[s], device_id=dev, device_id_type=MESH)

    def go(c, when=None):
        make = c if callable(c) else lambda: c
        pending.append((when, make))
        if when is None:
            make().start()
        else:
            @pl.when(when)
            def _():
                make().start()

    def come(c, when=None):
        if when is None:
            c.wait_recv()
        else:
            @pl.when(when)
            def _():
                c.wait_recv()

    phase("start")
    rank = [rank_of(l, 0) for l in range(4)]
    loads = {}

    def load(name, src, dst):
        c = pltpu.make_async_copy(src, dst, local.at[len(loads)])
        loads[name] = c
        c.start()

    def need(*names):
        for name in names:
            loads[name].wait()

    load("order", order_in.at[0, 0], order_row)
    load("t0", t0_in.at[0, 0], t0)
    load("g0", g0_in.at[0, 0], g0)
    load("rhs", rhs_in.at[0, 0], rhs)
    load("t1", t1_in.at[0, 0], tg1.at[rank[1]])
    load("k0", k0_in.at[0, 0], k0)
    load("g1", g1_in.at[0, 0], g1)
    load("t2", t2_in.at[0, 0], mid.at[0, rank[2]])
    load("g2", g2_in.at[0, 0], mid.at[1, rank[2]])
    load("k2", k2_in.at[0, 0], mid.at[pl.ds(2, 5), rank[2]])
    load("t3", t3_in.at[0, 0], top.at[0, rank[3]])
    load("g3", g3_in.at[0, 0], top.at[1, rank[3]])
    load("root", root_in.at[0, 0], top.at[2, rank[3]])
    load("k3", k3_in.at[0, 0, pl.ds(0, kinds)], top.at[pl.ds(3, kinds), rank[3]])
    load("k1", k1_in.at[0, 0], k1)

    barrier = pltpu.get_barrier_semaphore()
    for m in range(1, 8):
        pl.semaphore_signal(barrier, 1, device_id=member(m), device_id_type=MESH)
    total = jnp.int32(7)
    greeted = set()
    for level in range(4):
        for k in has[level]:
            key = (k, REACH[level][0] if k < 3 else REACH[level][1])
            if key in greeted:
                continue
            greeted.add(key)
            there, dev = neighbour(level, k)

            @pl.when(there)
            def _():
                pl.semaphore_signal(barrier, 1, device_id=dev, device_id_type=MESH)
            total = total + there.astype(jnp.int32)

    for level in range(2):
        for k in (1, 2, 3, 4):
            there, _ = neighbour(level, k)

            @pl.when(jnp.logical_not(there))
            def _():
                ybuf[level, k * skel:(k + 1) * skel, :] = jnp.zeros((skel, rhs_count), F32)
                qrecv[level, k - 1] = jnp.zeros((skel, rhs_count), F32)
    turned[...] = jnp.zeros_like(turned)

    chunks = range((top.shape[0] + 1) // 2)
    slots_own, slots_in, slots_on = ([slot() for _ in chunks] for _ in range(3))
    slots_mate = [slot() for _ in range(4)]

    def chunk_copy(c, block, dev, s):
        at = pl.ds(2 * c, min(2, top.shape[0] - 2 * c))
        return rcopy(top.at[at, block], top.at[at, block], s, dev)

    def mate_copy(n, mine):
        block = rank_of(3, (0, 1, 5, 4)[n] ^ (0 if mine else 2))
        return rcopy(top.at[:, block], top.at[:, block], slots_mate[n], member(2))

    def outer_send(c):
        go(chunk_copy(c, rank[3], member(1), slots_own[c]), outer)

    def inner_send():
        for c in chunks:
            go(chunk_copy(c, rank[3], member(5), slots_in[c]), inner)

    def inner_forward(c):
        come(chunk_copy(c, rank_of(3, 1), member(1), slots_own[c]), inner)
        go(chunk_copy(c, rank_of(3, 1), member(5), slots_on[c]), inner)

    def mate_send(n):
        for c in chunks:
            if n == 2:
                come(chunk_copy(c, rank_of(3, 5), member(5), slots_in[c]), inner)
            if n == 3:
                come(chunk_copy(c, rank_of(3, 4), member(5), slots_on[c]), inner)
        go(lambda: mate_copy(n, True), inner)

    near = [None, None, None] + [neighbour(2, k)[0] for k in (1, 2, 3, 4)]
    slots_mid = [slot() for _ in near]
    slots_mid_own = [slot() for _ in near]
    slots_mid_on = [slot() for _ in near]

    near_in = [inner if there is None else jnp.logical_and(inner, there) for there in near]
    near_out = [outer if there is None else jnp.logical_and(outer, there) for there in near]

    def mid_copy(n, m, to, s):
        block = rank_of(2, m)
        return rcopy(mid.at[n, block], mid.at[n, block], s, member(to))

    def used(n):
        return n < 3 or n - 2 in has[2]

    def mid_send(*wanted):
        for n in filter(used, wanted):
            go(mid_copy(n, 0, 1, slots_mid[n]), near_in[n])

    def mid_share(*wanted):
        for n in filter(used, wanted):
            go(mid_copy(n, 0, 2, slots_mid_own[n]), near_out[n])

    def mid_forward(*wanted):
        for n in filter(used, wanted):
            come(mid_copy(n, 1, 1, slots_mid[n]), near_out[n])
            go(lambda n=n: mid_copy(n, 1, 2, slots_mid_on[n]), near_out[n])

    def mid_full(n):
        come(mid_copy(n, 2, 2, slots_mid_own[n]), near[n])
        come(mid_copy(n, 3, 2, slots_mid_on[n]), near[n])

    def onehot_pt(level):
        lanes = lax.broadcasted_iota(jnp.int32, (box, box), 1)
        return jnp.where(lanes == order_col[:, level:level + 1], 1.0, 0.0).astype(BF16)

    def onehot_p(level):
        rows = lax.broadcasted_iota(jnp.int32, (box, box), 0)
        return jnp.where(rows == order_row[level:level + 1, :], 1.0, 0.0).astype(BF16)

    def make_n(level):
        if level == 0:
            need("t0", "g0")
            n0[:skel, :] = -dot3(t0[...], g0[...], NN)
            n0[skel:, :] = g0[...]
            return
        need("g1")
        n1[:, :skel] = -dot3(g1[...], tg1[...].reshape(skel, skel), NN)
        n1[:, skel:] = g1[...]

    need("order")
    order_f = order_row[...].astype(F32)
    order_f = jnp.concatenate([order_f, jnp.zeros((8 - order_f.shape[0], box), F32)], axis=0)
    order_col[...] = order_f.T.astype(jnp.int32)

    phase("f0_make")
    make_n(0)
    phase("f0_a")
    need("rhs")
    abuf[...] = pick_left(onehot_pt(0), rhs[...], NT)
    phase("f0_y")
    y_own = dot3(n0[...], abuf[...], TN)
    ybuf[0, :skel, :] = y_own
    ypart[0] = y_own
    phase("f0_barrier")
    pl.semaphore_wait(barrier, total)
    phase("f0_send")
    slots_y0 = {k: slot() for k in has[0]}
    for k in along[0] + cross[0]:
        there, dev = neighbour(0, k)
        far = OPPOSITE[k]
        go(rcopy(ypart.at[0], ybuf.at[0, pl.ds(far * skel, skel), :], slots_y0[k], dev), there)
    need("t1")
    t1_copy = rcopy(tg1.at[rank[1]], tg1.at[rank[1]], slot(), member(1))
    go(t1_copy)
    need("t3", "g3", "root", "k3")
    inner_send()
    mate_send(0)
    phase("f0_s")
    need("k0")
    s_own = abuf[:skel, :] - dot3(k0[0], ypart[0], TN)
    ptbuf[...] = onehot_pt(1)
    for k in cross[0] + along[0]:
        there, dev = neighbour(0, k)
        phase(f"f0_wait{k}")
        come(rcopy(ypart.at[0], ybuf.at[0, pl.ds(k * skel, skel), :], slots_y0[OPPOSITE[k]], dev), there)
        phase(f"f0_s{k}")
        s_own = s_own - dot3(k0[k], ybuf[0, k * skel:(k + 1) * skel, :], TN)
    ssend[0] = s_own
    vbuf[span(rank[1], skel), :] = s_own
    give = rcopy(ssend.at[0], vbuf.at[span(rank[1], skel), :], slot(), member(1))
    go(give)
    need("t2", "g2", "k2")
    mid_send(0)
    mid_share(*range(7))
    outer_send(0)
    base0[:skel, :] = -dot3(t0[...], ypart[0], NN)
    base0[skel:, :] = ypart[0]
    phase("f0_n1")
    come(t1_copy)
    make_n(1)
    phase("f0_gwait")
    come(give)

    phase("f1_a")
    cols = skel >> 1
    rows = span(rank[1], cols)
    abuf[...] = pick_left(ptbuf[...], vbuf[...], NN)
    phase("f1_y")
    y_own = dot3(n1[...], abuf[...], NN)
    ypart[1, :cols, :] = y_own
    ybuf[1, rows, :] = y_own

    def at(k, m):
        return ybuf.at[1, pl.ds(pl.multiple_of(k * skel + rank_of(1, m) * cols, cols), cols), :]

    own_src = ypart.at[1, pl.ds(0, cols), :]
    s_a = slot()
    s_c = {k: [slot(), slot()] for k in cross[1]}
    s_b = {k: slot() for k in along[1]}
    s_d = {k: slot() for k in along[1]}
    phase("f1_send")
    mate = rcopy(own_src, at(0, 0), s_a, member(1))
    go(mate)
    for k in along[1]:
        there, dev = neighbour(1, k)
        go(rcopy(own_src, at(OPPOSITE[k], 0), s_b[k], dev), there)
    for k in cross[1]:
        there, dev = neighbour(1, k)
        go(rcopy(own_src, at(OPPOSITE[k], 0), s_c[k][0], dev), there)
    mid_send(1)
    outer_send(1)
    base1[:skel, :] = -dot3(tg1[rank[1]], y_own, TN)
    base1[skel:, :] = jnp.zeros((skel, rhs_count), F32)
    base1[pl.ds(pl.multiple_of(skel + rank[1] * cols, cols), cols), :] = y_own
    phase("f1_ywait")
    come(mate)
    for k in cross[1]:
        there, dev = neighbour(1, k)
        go(rcopy(at(0, 1), at(OPPOSITE[k], 1), s_c[k][1], dev), there)
    inner_forward(0)
    mid_forward(0)
    phase("f1_s0")
    need("k1")
    s_own = abuf[rows, :] - dot3(k1[0], ybuf[1, :skel, :], NN)
    phase("f1_relay")
    for k in cross[1]:
        there, dev = neighbour(1, k)
        come(rcopy(own_src, at(k, 0), s_c[OPPOSITE[k]][0], dev), there)
    for k in along[1]:
        there, dev = neighbour(1, k)
        come(rcopy(own_src, at(k, 0), s_b[OPPOSITE[k]], dev), there)
        go(rcopy(at(k, 0), at(k, 0), s_d[k], member(1)), there)
    mid_send(2)
    for k in cross[1]:
        there, dev = neighbour(1, k)
        phase(f"f1_cross{k}")
        come(rcopy(own_src, at(k, 1), s_c[OPPOSITE[k]][1], dev), there)
        s_own = s_own - dot3(k1[k], ybuf[1, k * skel:(k + 1) * skel, :], NN)
    for k in along[1]:
        there, dev = neighbour(1, k)
        phase(f"f1_along{k}")
        come(rcopy(at(k, 1), at(k, 1), s_d[k], member(1)), there)
        s_own = s_own - dot3(k1[k], ybuf[1, k * skel:(k + 1) * skel, :], NN)
    turned[:, :cols] = s_own.T

    phase("l2_send")
    s_t2 = [slot() for _ in range(4)]
    half_of = lambda m: span(flipped(1, m), half)
    go(rcopy(turned.at[half_of(1)], v2.at[rank[2]], s_t2[1], member(1)), inner)
    go(rcopy(turned.at[half_of(3)], v2.at[rank[2]], s_t2[3], member(3)), inner)
    go(rcopy(turned.at[half_of(2)], v2.at[rank[2]], s_t2[2], member(2)), outer)
    mid_send(3, 4, 5, 6)
    outer_send(2)
    inner_forward(1)
    inner_forward(2)

    def wide_pick(pick, level, width, lanes):
        o = order_row[level:level + 1, :]
        o = o + sum((lanes - width) * (o >= width * b).astype(jnp.int32) for b in range(1, box // width))
        lines = lax.broadcasted_iota(jnp.int32, pick.shape, 0)
        pick[...] = jnp.where(lines == o, 1.0, 0.0).astype(BF16)

    def beside(k):
        there, (to_i, to_j) = neighbour(2, k)
        if k > 2:
            step = 1 + 2 * (1 - bits[2]) if k == 4 else -(1 + 2 * bits[2])
            to_i, to_j = i, j + step
        return there, (to_i, to_j)

    s_y2 = {k: slot() for k in has[2]}
    s_q2 = {k: slot() for k in has[2]}
    s_t3 = {m: slot() for m in (1, 4)}
    s_x3 = {m: slot() for m in (1, 4)}
    s_x2 = {m: slot() for m in (1, 2, 3)}
    s_y3 = {k: slot() for k in has[3]}
    s_q3 = {k: slot() for k in has[3]}
    quarter_of = lambda m: span(flipped(2, m), share)
    y2_copy = lambda k: rcopy(y2, yr2.at[OPPOSITE[k] - 1], s_y2[k], beside(k)[1])
    q2_copy = lambda k: rcopy(q2.at[k - 1], qr2.at[OPPOSITE[k] - 1], s_q2[k], beside(k)[1])
    y3_copy = lambda k: rcopy(y3, yr3.at[OPPOSITE[k] - 1], s_y3[k], neighbour(3, k)[1])
    q3_copy = lambda k: rcopy(q3.at[k - 1], qr3.at[OPPOSITE[k] - 1], s_q3[k], neighbour(3, k)[1])
    up_copy = lambda m: rcopy(turn2.at[quarter_of(m)], v3.at[bits[2]], s_t3[m], member(m))
    down_copy = lambda m: rcopy(x3.at[flipped(2, m)], t2.at[quarter_of(0)], s_x3[m], member(m))
    out_copy = lambda m: rcopy(x2.at[rank_of(2, m)], back2.at[half_of(0)], s_x2[m], member(m))

    @pl.when(outer)
    def _():
        phase("l2_pick")
        wide_pick(pick2, 2, cols, turned.shape[1])
        mid_forward(1)
        v2[rank[2]] = turned[half_of(0), :]
        phase("l2_in")
        come(rcopy(turned.at[half_of(0)], v2.at[rank_of(2, 2)], s_t2[2], member(2)))
        come(rcopy(turned.at[half_of(0)], v2.at[rank_of(2, 1)], s_t2[1], member(1)))
        come(rcopy(turned.at[half_of(0)], v2.at[rank_of(2, 3)], s_t2[3], member(3)))
        phase("l2_a")
        full = lambda n: mid[n].reshape(skel, skel)
        a = pick_right(jnp.concatenate([v2[b] for b in range(4)], axis=1), pick2[...], NN)
        s0, r0 = a[:, :skel], a[:, skel:]
        phase("l2_y")
        mid_full(0)
        mid_full(1)
        y = dot3(r0 - dot3(s0, full(0), NT), full(1), NT)
        y2[...] = y
        for k in has[2]:
            @pl.when(beside(k)[0])
            def _():
                y2_copy(k).start()
        phase("l2_s")
        mid_forward(2)
        mid_full(2)
        turn2[...] = s0 - dot3(y, full(2), NT)
        for k in has[2]:
            mid_forward(2 + k)
        for k in has[2]:
            phase(f"l2_s{k}")

            @pl.when(beside(k)[0])
            def _():
                mid_full(2 + k)
                rcopy(y2, yr2.at[k - 1], s_y2[OPPOSITE[k]], beside(k)[1]).wait_recv()
                turn2[...] = turn2[...] - dot3(yr2[k - 1], full(2 + k), NT)
        for m in (4, 1):
            up_copy(m).start()
        phase(None)

    @pl.when(inner)
    def _():
        phase("l3_pick")
        wide_pick(pick3, 3, skel, skel)
        for n in (1, 2, 3):
            mate_send(n)
        for n in range(4):
            come(mate_copy(n, False))
        phase("l3_in")
        for m in (1, 4):
            come(rcopy(turn2.at[quarter_of(0)], v3.at[flipped(2, m)], s_t3[m], member(m)))
        full = lambda n: top[n].reshape(skel, skel)
        phase("l3_y")
        a = pick_right(jnp.concatenate([v3[0], v3[1]], axis=1), pick3[...], NN)
        s0, r0 = a[:, :skel], a[:, skel:]
        y = dot3(r0 - dot3(s0, full(0), NT), full(1), NT)
        y3[...] = y
        for k in has[3]:
            @pl.when(neighbour(3, k)[0])
            def _():
                y3_copy(k).start()
        phase("l3_s")
        v3[0] = s0 - dot3(y, full(3), NT)
        for k in has[3]:
            phase(f"l3_s{k}")

            @pl.when(neighbour(3, k)[0])
            def _():
                rcopy(y3, yr3.at[k - 1], s_y3[OPPOSITE[k]], neighbour(3, k)[1]).wait_recv()
                v3[0] = v3[0] - dot3(yr3[k - 1], full(3 + k), NT)
        phase("l3_q")
        t = dot3(v3[0], full(2), NT)
        for k in has[3]:
            @pl.when(neighbour(3, k)[0])
            def _():
                q3[k - 1] = dot3(t, full(3 + k), NN)
                q3_copy(k).start()
        v3[0] = dot3(t, full(3), NN)
        for k in has[3]:
            phase(f"l3_u{k}")

            @pl.when(neighbour(3, k)[0])
            def _():
                rcopy(q3.at[k - 1], qr3.at[k - 1], s_q3[OPPOSITE[k]], neighbour(3, k)[1]).wait_recv()
                v3[0] = v3[0] + qr3[k - 1]
        phase("l3_x")
        xr = y - dot3(v3[0], full(1), NN)
        xs = t - dot3(xr, full(0), NN)
        xv = pick_right(jnp.concatenate([xs, xr], axis=1), pick3[...], NT)
        x3[0], x3[1] = xv[:, :skel], xv[:, skel:]
        for m in (4, 1):
            down_copy(m).start()
        phase(None)

    @pl.when(outer)
    def _():
        phase("l2_tin")
        for m in (1, 4):
            come(rcopy(x3.at[bits[2]], t2.at[quarter_of(m)], s_x3[m], member(m)))
        full = lambda n: mid[n].reshape(skel, skel)
        phase("l2_q")
        t = t2[...]
        for k in reversed(has[2]):
            @pl.when(beside(k)[0])
            def _():
                q2[k - 1] = dot3(t, full(2 + k), NN)
                q2_copy(k).start()
        yr2[0] = dot3(t, full(2), NN)
        for k in has[2]:
            phase(f"l2_u{k}")

            @pl.when(beside(k)[0])
            def _():
                rcopy(q2.at[k - 1], qr2.at[k - 1], s_q2[OPPOSITE[k]], beside(k)[1]).wait_recv()
                yr2[0] = yr2[0] + qr2[k - 1]
        phase("l2_x")
        xr = y2[...] - dot3(yr2[0], full(1), NN)
        xs = t - dot3(xr, full(0), NN)
        xv = pick_right(jnp.concatenate([xs, xr], axis=1), pick2[...], NT)
        wide = turned.shape[1]
        for b in range(4):
            x2[b] = xv[:, b * wide:(b + 1) * wide]
        for m in (3, 1, 2):
            out_copy(m).start()
        back2[half_of(0), :] = x2[rank[2]]
        phase(None)

    phase("l2_out")
    ptbuf[...] = onehot_p(1)
    come(rcopy(x2.at[rank[2]], back2.at[half_of(2)], s_x2[2], member(2)), outer)
    for m in (1, 3):
        come(rcopy(x2.at[rank[2]], back2.at[half_of(m)], s_x2[m], member(m)), inner)
    t_own = back2[...].T[:skel >> 1]

    for level in (1, 0):
        phase(f"b{level}_q")
        cols = skel >> level
        rows = span(rank[level], cols)
        s_q = {k: slot() for k in has[level]}
        for k in along[level] + cross[level]:
            at_k = pl.ds(k * skel, skel)
            qsend[level, at_k, :] = dot3(k1[k], t_own, TN) if level else dot3(k0[k], t_own, NN)
            there, dev = neighbour(level, k)
            go(rcopy(qsend.at[level, at_k, :], qrecv.at[level, OPPOSITE[k] - 1], s_q[k], dev), there)
        u = dot3(k1[0], t_own, TN) if level else dot3(k0[0], t_own, NN)
        phase(f"b{level}_t")
        if level == 0:
            abuf[...] = base0[...]
            abuf[:skel, :] = abuf[:skel, :] + t_own
            ptbuf[...] = onehot_pt(0)
        else:
            abuf[...] = base1[...]
            abuf[rows, :] = abuf[rows, :] + t_own
        for k in cross[level] + along[level]:
            phase(f"b{level}_wait{k}")
            there, dev = neighbour(level, k)
            come(rcopy(qsend.at[level, pl.ds(k * skel, skel), :], qrecv.at[level, k - 1], s_q[OPPOSITE[k]], dev), there)
        phase(f"b{level}_u")
        u = u + ((qrecv[level, 0] + qrecv[level, 1]) + (qrecv[level, 2] + qrecv[level, 3]))
        if level > 0:
            qsend[level, :skel, :] = u
            c = rcopy(qsend.at[level, span(rank_of(level, 1), cols), :], urecv1.at[0], slot(), member(1))
            go(c)
            come(c)
            u = qsend[level, rows, :] + urecv1[0]
        phase(f"b{level}_comb")
        abuf[...] = abuf[...] - (dot3(n1[...], u, TN) if level else dot3(n0[...], u, NN))
        phase(f"b{level}_x")
        if level > 0:
            xpart[...] = pick_left(ptbuf[...], abuf[...], NN)
            c = rcopy(xpart.at[span(rank_of(level, 1), skel), :], xrecv1.at[0], slot(), member(1))
            go(c)
            phase(f"b{level}_xwait")
            come(c)
            t_own = xpart[span(rank[level], skel), :] + xrecv1[0]
        else:
            ch, cl = halves(abuf[...])
            pt = ptbuf[...]
            out[0, 0] = product(ch, pt, TN) + product(cl, pt, TN)

    phase("drain")
    for when, make in pending:
        if when is None:
            make().wait_send()
        else:
            @pl.when(when)
            def _():
                make().wait_send()

    @pl.when(inner)
    def _():
        for k in has[3]:
            @pl.when(neighbour(3, k)[0])
            def _():
                y3_copy(k).wait_send()
                q3_copy(k).wait_send()
        for m in (4, 1):
            down_copy(m).wait_send()

    @pl.when(outer)
    def _():
        for k in has[2]:
            @pl.when(beside(k)[0])
            def _():
                y2_copy(k).wait_send()
                q2_copy(k).wait_send()
        for m in (4, 1):
            up_copy(m).wait_send()
        for m in (3, 1, 2):
            out_copy(m).wait_send()
    phase(None)


def body(size_x, size_y, right_sides, skeleton_order, *weights):
    rows = right_sides.shape[2]
    box = right_sides.shape[3]
    skel = box // 2
    weights = [jnp.swapaxes(w, -1, -2) if w.shape[-1] < skel else w for w in weights]
    vm = lambda *shape: pltpu.VMEM(shape, F32)
    widths = [skel >> level for level in range(4)]
    half, share = rows // 2, rows // 4
    kinds = 5 if size_y > REACH[3][1] else 3
    lanes = -(-widths[1] // 128) * 128
    scratch = [
        vm(rows, box), pltpu.VMEM((4, box), jnp.int32), vm(skel, skel), vm(2, widths[1], skel),
        vm(skel, skel), vm(widths[1], skel), vm(5, skel, skel), vm(5, widths[1], skel),
        vm(2, 5 * skel, rows), vm(box, rows), vm(2, 5 * skel, rows), vm(2, 4, skel, rows),
        vm(1, widths[1], rows), vm(1, skel, rows), vm(box, rows), vm(box, rows), vm(box, rows),
        vm(box, skel), vm(widths[1], box),
        vm(box, rows), vm(2, skel, rows), vm(1, skel, rows),
        pltpu.VMEM((box, box), BF16), pltpu.VMEM((box, 8), jnp.int32),
        vm(7, 4, widths[2], skel), vm(rows, lanes), vm(4, half, lanes),
        vm(half, skel), vm(4, half, skel), vm(4, half, skel), vm(4, half, skel),
        vm(4, half, lanes), vm(rows, lanes), pltpu.VMEM((4 * lanes, box), BF16), vm(half, skel), vm(half, skel),
        vm(3 + kinds, 8, widths[3], skel), vm(2, share, skel),
        vm(share, skel), vm(kinds - 1, share, skel), vm(kinds - 1, share, skel), vm(kinds - 1, share, skel),
        vm(2, share, skel), pltpu.VMEM((box, box), BF16),
        pltpu.SemaphoreType.DMA((16,)),
        pltpu.SemaphoreType.DMA((128,)), pltpu.SemaphoreType.DMA((128,)),
    ]
    return pl.pallas_call(
        functools.partial(kernel, size_x, size_y),
        out_shape=jax.ShapeDtypeStruct(right_sides.shape, F32),
        in_specs=[pl.BlockSpec(memory_space=pl.ANY)] * (2 + len(weights)),
        out_specs=pl.BlockSpec(memory_space=pltpu.VMEM),
        scratch_shapes=scratch,
        compiler_params=pltpu.CompilerParams(
            collective_id=0, has_side_effects=True, vmem_limit_bytes=60 * 2**20
        ),
    )(right_sides, skeleton_order, *weights)


def solution(mesh):
    four = P("bx", "by", None, None)
    five = P("bx", "by", None, None, None)
    in_specs = (four,) * 10 + (five,) * 4 + (four,)
    return jax.shard_map(
        functools.partial(body, mesh.shape["bx"], mesh.shape["by"]),
        mesh=mesh, in_specs=in_specs, out_specs=four, check_vma=False,
    )
```

time: 133 us -> 120 us (0.902)
  Pallas kernels: 131 us -> 118 us
    pallas_call x1, Pallas kernels: 131 us -> 118 us  [body(): pl.pallas_call(functools.partial(kernel, size_x, size_y), out_shape=jax.S...]
where the time goes in v3:
time: 120 us; the launch traced here: 119 us
  Pallas kernels  118 us (98%)
  local copies, waits for them, and re-layouts  1.77 us (1%)
    pallas_call x1, Pallas kernels, body(): pl.pallas_call(functools.partial(kernel, size_x, size_y), out_shape=jax.S...  118 us

profile of v3, /device:TPU:1, one launch (start us, length us, event | category | flops | bytes accessed | tf_op | source)
XLA Modules:
  0.0 119.4 jit_solution(17624141230245934885)
XLA Ops:
  0.0 117.6 %shard_map.145 = f32[1,1,128,768]{3,2,1,0:T(8,128)} custom-call(f32[1,1,128,768]{3,2,1,0:T(8,128)} %refs_0_.1, s32[1,1,4,768]{3,2,1,0:T(4,128)} %refs_1_.1, f32[1,1,384,384]{3,2,1,0:T(8,128)} %refs_2_.1, f32[1,1,192,384]{3,2,1,0:T(8,128)} %bitcast.13, f32[1,1,96,384]{3,2,1,0:T(8,128)} %bitcast.15, f32[1,1,48,384]{3,2,1,0:T(8,128)} %bitcast.17, ...), custom_call_target="tpu_custom_call" | custom-call | tf_op jit(solution)/shard_map/pallas_call | solution.py:668
  117.6 1.8 %copy.17 = f32[1,1,128,768]{3,2,1,0:T(8,128)} copy(f32[1,1,128,768]{3,2,1,0:T(8,128)} %shard_map.145) | data formatting | bytes 786432

commit v4 on v3

--- a/solution.py
+++ b/solution.py
@@ -32,14 +32,36 @@
     return product(ah, bh, dims) + (product(ah, bl, dims) + product(al, bh, dims))
 
 
+def lanes_summed(x):
+    wide = x.shape[1] // 2
+    return x[:, :wide] + x[:, wide:]
+
+
+def rows_summed(x):
+    tall = x.shape[0] // 2
+    return x[:tall] + x[tall:]
+
+
+def dot_left(a, b, dims):
+    ah, al = halves(a)
+    bh, bl = halves(b)
+    return lanes_summed(product(ah, jnp.concatenate([bh, bl], axis=1), dims)) + product(al, bh, dims)
+
+
+def dot_right(a, b, dims):
+    ah, al = halves(a)
+    bh, bl = halves(b)
+    return rows_summed(product(jnp.concatenate([ah, al], axis=0), bh, dims)) + product(ah, bl, dims)
+
+
 def pick_left(onehot, b, dims):
-    bh, bl = halves(b)
-    return product(onehot, bh, dims) + product(onehot, bl, dims)
+    return lanes_summed(product(onehot, jnp.concatenate(halves(b), axis=1 if dims == NN else 0), dims))
 
 
 def pick_right(a, onehot, dims):
-    ah, al = halves(a)
-    return product(ah, onehot, dims) + product(al, onehot, dims)
+    if dims == TN:
+        return rows_summed(product(jnp.concatenate(halves(a), axis=1), onehot, dims))
+    return rows_summed(product(jnp.concatenate(halves(a), axis=0), onehot, dims))
 
 
 class Phases:
@@ -58,8 +80,8 @@
     (rhs_in, order_in, t0_in, t1_in, t2_in, t3_in, g0_in, g1_in, g2_in, g3_in,
      k0_in, k1_in, k2_in, k3_in, root_in, out) = refs[:16]
     (rhs, order_row, t0, tg1, g0, g1, k0, k1,
-     ybuf, vbuf, qsend, qrecv, urecv1, xrecv1, xpart, base0, base1,
-     n0, n1, abuf, ypart, ssend, ptbuf, order_col,
+     ybuf, vbuf, qsend, qrecv, urecv1, xrecv1, xpart, base1,
+     n1, abuf, ypart, ssend, ptbuf, order_col, wbuf, wpart, kmate, kturn, krows, tfull, nsend, nrecv,
      mid, turned, v2, y2, yr2, q2, qr2, x2, back2, pick2, turn2, t2,
      top, v3, y3, yr3, q3, qr3, x3, pick3, local, send, recv) = refs[16:]
     skel = t0.shape[0]
@@ -185,6 +207,12 @@
             def _():
                 ybuf[level, k * skel:(k + 1) * skel, :] = jnp.zeros((skel, rhs_count), F32)
                 qrecv[level, k - 1] = jnp.zeros((skel, rhs_count), F32)
+    for k in along[1]:
+        there, _ = neighbour(1, k)
+
+        @pl.when(jnp.logical_not(there))
+        def _():
+            nrecv[k - 3] = jnp.zeros(nrecv.shape[1:], F32)
     turned[...] = jnp.zeros_like(turned)
 
     chunks = range((top.shape[0] + 1) // 2)
@@ -258,28 +286,17 @@
         rows = lax.broadcasted_iota(jnp.int32, (box, box), 0)
         return jnp.where(rows == order_row[level:level + 1, :], 1.0, 0.0).astype(BF16)
 
-    def make_n(level):
-        if level == 0:
-            need("t0", "g0")
-            n0[:skel, :] = -dot3(t0[...], g0[...], NN)
-            n0[skel:, :] = g0[...]
-            return
-        need("g1")
-        n1[:, :skel] = -dot3(g1[...], tg1[...].reshape(skel, skel), NN)
-        n1[:, skel:] = g1[...]
-
     need("order")
     order_f = order_row[...].astype(F32)
     order_f = jnp.concatenate([order_f, jnp.zeros((8 - order_f.shape[0], box), F32)], axis=0)
     order_col[...] = order_f.T.astype(jnp.int32)
 
-    phase("f0_make")
-    make_n(0)
     phase("f0_a")
     need("rhs")
     abuf[...] = pick_left(onehot_pt(0), rhs[...], NT)
     phase("f0_y")
-    y_own = dot3(n0[...], abuf[...], TN)
+    need("t0", "g0")
+    y_own = dot_left(g0[...], abuf[skel:, :] - dot_left(t0[...], abuf[:skel, :], TN), TN)
     ybuf[0, :skel, :] = y_own
     ypart[0] = y_own
     phase("f0_barrier")
@@ -290,44 +307,47 @@
         there, dev = neighbour(0, k)
         far = OPPOSITE[k]
         go(rcopy(ypart.at[0], ybuf.at[0, pl.ds(far * skel, skel), :], slots_y0[k], dev), there)
-    need("t1")
-    t1_copy = rcopy(tg1.at[rank[1]], tg1.at[rank[1]], slot(), member(1))
-    go(t1_copy)
-    need("t3", "g3", "root", "k3")
+    need("t2", "g2", "k2", "t3", "g3", "root", "k3")
+    mid_send(0)
+    outer_send(0)
     inner_send()
     mate_send(0)
     phase("f0_s")
     need("k0")
-    s_own = abuf[:skel, :] - dot3(k0[0], ypart[0], TN)
+    s_own = abuf[:skel, :] - dot_left(k0[0], ypart[0], TN)
     ptbuf[...] = onehot_pt(1)
     for k in cross[0] + along[0]:
         there, dev = neighbour(0, k)
         phase(f"f0_wait{k}")
         come(rcopy(ypart.at[0], ybuf.at[0, pl.ds(k * skel, skel), :], slots_y0[OPPOSITE[k]], dev), there)
         phase(f"f0_s{k}")
-        s_own = s_own - dot3(k0[k], ybuf[0, k * skel:(k + 1) * skel, :], TN)
+        s_own = s_own - dot_left(k0[k], ybuf[0, k * skel:(k + 1) * skel, :], TN)
     ssend[0] = s_own
     vbuf[span(rank[1], skel), :] = s_own
     give = rcopy(ssend.at[0], vbuf.at[span(rank[1], skel), :], slot(), member(1))
     go(give)
-    need("t2", "g2", "k2")
-    mid_send(0)
+    mid_send(1)
+    outer_send(1)
     mid_share(*range(7))
-    outer_send(0)
-    base0[:skel, :] = -dot3(t0[...], ypart[0], NN)
-    base0[skel:, :] = ypart[0]
-    phase("f0_n1")
-    come(t1_copy)
-    make_n(1)
     phase("f0_gwait")
+    need("t1", "g1", "k1")
     come(give)
 
     phase("f1_a")
     cols = skel >> 1
     rows = span(rank[1], cols)
     abuf[...] = pick_left(ptbuf[...], vbuf[...], NN)
+    phase("f1_w")
+    w_own = abuf[pl.ds(pl.multiple_of(skel + rank[1] * cols, cols), cols), :] - dot_left(tg1[rank[1]], abuf[:skel, :], NN)
+    wpart[...] = w_own
+    wbuf[rows, :] = w_own
+    give_w = rcopy(wpart, wbuf.at[rows, :], slot(), member(1))
+    go(give_w)
+    ptbuf[...] = onehot_p(1)
+    phase("f1_wwait")
+    come(give_w)
     phase("f1_y")
-    y_own = dot3(n1[...], abuf[...], NN)
+    y_own = dot_left(g1[...], wbuf[...], NN)
     ypart[1, :cols, :] = y_own
     ybuf[1, rows, :] = y_own
 
@@ -348,9 +368,9 @@
     for k in cross[1]:
         there, dev = neighbour(1, k)
         go(rcopy(own_src, at(OPPOSITE[k], 0), s_c[k][0], dev), there)
-    mid_send(1)
-    outer_send(1)
-    base1[:skel, :] = -dot3(tg1[rank[1]], y_own, TN)
+    mid_send(2)
+    outer_send(2)
+    base1[:skel, :] = -dot_left(tg1[rank[1]], y_own, TN)
     base1[skel:, :] = jnp.zeros((skel, rhs_count), F32)
     base1[pl.ds(pl.multiple_of(skel + rank[1] * cols, cols), cols), :] = y_own
     phase("f1_ywait")
@@ -361,8 +381,7 @@
     inner_forward(0)
     mid_forward(0)
     phase("f1_s0")
-    need("k1")
-    s_own = abuf[rows, :] - dot3(k1[0], ybuf[1, :skel, :], NN)
+    s_own = abuf[rows, :] - dot_left(k1[0], ybuf[1, :skel, :], NN)
     phase("f1_relay")
     for k in cross[1]:
         there, dev = neighbour(1, k)
@@ -371,17 +390,17 @@
         there, dev = neighbour(1, k)
         come(rcopy(own_src, at(k, 0), s_b[OPPOSITE[k]], dev), there)
         go(rcopy(at(k, 0), at(k, 0), s_d[k], member(1)), there)
-    mid_send(2)
+    mid_send(3)
     for k in cross[1]:
         there, dev = neighbour(1, k)
         phase(f"f1_cross{k}")
         come(rcopy(own_src, at(k, 1), s_c[OPPOSITE[k]][1], dev), there)
-        s_own = s_own - dot3(k1[k], ybuf[1, k * skel:(k + 1) * skel, :], NN)
+        s_own = s_own - dot_left(k1[k], ybuf[1, k * skel:(k + 1) * skel, :], NN)
     for k in along[1]:
         there, dev = neighbour(1, k)
         phase(f"f1_along{k}")
         come(rcopy(at(k, 1), at(k, 1), s_d[k], member(1)), there)
-        s_own = s_own - dot3(k1[k], ybuf[1, k * skel:(k + 1) * skel, :], NN)
+        s_own = s_own - dot_left(k1[k], ybuf[1, k * skel:(k + 1) * skel, :], NN)
     turned[:, :cols] = s_own.T
 
     phase("l2_send")
@@ -390,8 +409,12 @@
     go(rcopy(turned.at[half_of(1)], v2.at[rank[2]], s_t2[1], member(1)), inner)
     go(rcopy(turned.at[half_of(3)], v2.at[rank[2]], s_t2[3], member(3)), inner)
     go(rcopy(turned.at[half_of(2)], v2.at[rank[2]], s_t2[2], member(2)), outer)
-    mid_send(3, 4, 5, 6)
-    outer_send(2)
+    mid_send(4, 5, 6)
+    t1_copy = rcopy(tg1.at[rank[1]], tg1.at[rank[1]], slot(), member(1))
+    go(t1_copy)
+    mate_k = {k: rcopy(k1.at[k], kmate.at[k - 3], slot(), member(1)) for k in along[1]}
+    for k in along[1]:
+        go(mate_k[k], neighbour(1, k)[0])
     inner_forward(1)
     inner_forward(2)
 
@@ -422,7 +445,7 @@
     q3_copy = lambda k: rcopy(q3.at[k - 1], qr3.at[OPPOSITE[k] - 1], s_q3[k], neighbour(3, k)[1])
     up_copy = lambda m: rcopy(turn2.at[quarter_of(m)], v3.at[bits[2]], s_t3[m], member(m))
     down_copy = lambda m: rcopy(x3.at[flipped(2, m)], t2.at[quarter_of(0)], s_x3[m], member(m))
-    out_copy = lambda m: rcopy(x2.at[rank_of(2, m)], back2.at[half_of(0)], s_x2[m], member(m))
+    out_copy = lambda m: rcopy(x2.at[flipped(1, m)], back2.at[half_of(0)], s_x2[m], member(m))
 
     @pl.when(outer)
     def _():
@@ -441,7 +464,7 @@
         phase("l2_y")
         mid_full(0)
         mid_full(1)
-        y = dot3(r0 - dot3(s0, full(0), NT), full(1), NT)
+        y = dot_right(r0 - dot_right(s0, full(0), NT), full(1), NT)
         y2[...] = y
         for k in has[2]:
             @pl.when(beside(k)[0])
@@ -450,7 +473,7 @@
         phase("l2_s")
         mid_forward(2)
         mid_full(2)
-        turn2[...] = s0 - dot3(y, full(2), NT)
+        turn2[...] = s0 - dot_right(y, full(2), NT)
         for k in has[2]:
             mid_forward(2 + k)
         for k in has[2]:
@@ -460,7 +483,7 @@
             def _():
                 mid_full(2 + k)
                 rcopy(y2, yr2.at[k - 1], s_y2[OPPOSITE[k]], beside(k)[1]).wait_recv()
-                turn2[...] = turn2[...] - dot3(yr2[k - 1], full(2 + k), NT)
+                turn2[...] = turn2[...] - dot_right(yr2[k - 1], full(2 + k), NT)
         for m in (4, 1):
             up_copy(m).start()
         phase(None)
@@ -480,29 +503,29 @@
         phase("l3_y")
         a = pick_right(jnp.concatenate([v3[0], v3[1]], axis=1), pick3[...], NN)
         s0, r0 = a[:, :skel], a[:, skel:]
-        y = dot3(r0 - dot3(s0, full(0), NT), full(1), NT)
+        y = dot_right(r0 - dot_right(s0, full(0), NT), full(1), NT)
         y3[...] = y
         for k in has[3]:
             @pl.when(neighbour(3, k)[0])
             def _():
                 y3_copy(k).start()
         phase("l3_s")
-        v3[0] = s0 - dot3(y, full(3), NT)
+        v3[0] = s0 - dot_right(y, full(3), NT)
         for k in has[3]:
             phase(f"l3_s{k}")
 
             @pl.when(neighbour(3, k)[0])
             def _():
                 rcopy(y3, yr3.at[k - 1], s_y3[OPPOSITE[k]], neighbour(3, k)[1]).wait_recv()
-                v3[0] = v3[0] - dot3(yr3[k - 1], full(3 + k), NT)
+                v3[0] = v3[0] - dot_right(yr3[k - 1], full(3 + k), NT)
         phase("l3_q")
-        t = dot3(v3[0], full(2), NT)
+        t = dot_right(v3[0], full(2), NT)
         for k in has[3]:
             @pl.when(neighbour(3, k)[0])
             def _():
-                q3[k - 1] = dot3(t, full(3 + k), NN)
+                q3[k - 1] = dot_right(t, full(3 + k), NN)
                 q3_copy(k).start()
-        v3[0] = dot3(t, full(3), NN)
+        v3[0] = dot_right(t, full(3), NN)
         for k in has[3]:
             phase(f"l3_u{k}")
 
@@ -511,17 +534,32 @@
                 rcopy(q3.at[k - 1], qr3.at[k - 1], s_q3[OPPOSITE[k]], neighbour(3, k)[1]).wait_recv()
                 v3[0] = v3[0] + qr3[k - 1]
         phase("l3_x")
-        xr = y - dot3(v3[0], full(1), NN)
-        xs = t - dot3(xr, full(0), NN)
+        xr = y - dot_right(v3[0], full(1), NN)
+        xs = t - dot_right(xr, full(0), NN)
         xv = pick_right(jnp.concatenate([xs, xr], axis=1), pick3[...], NT)
         x3[0], x3[1] = xv[:, :skel], xv[:, skel:]
         for m in (4, 1):
             down_copy(m).start()
         phase(None)
 
+    phase("b1_make")
+    come(t1_copy)
+    n1[:, :skel] = -dot3(g1[...], tg1[...].reshape(skel, skel), NN)
+    n1[:, skel:] = g1[...]
+    for k in along[1]:
+        there, _ = neighbour(1, k)
+
+        @pl.when(there)
+        def _():
+            mate_k[k].wait_recv()
+            for n, block in enumerate((k1[k], kmate[k - 3])):
+                kturn[...] = block.T
+                krows[k - 3, n] = kturn[rows, :]
+
     @pl.when(outer)
     def _():
         phase("l2_tin")
+        pick2[:box, :] = onehot_p(2)
         for m in (1, 4):
             come(rcopy(x3.at[bits[2]], t2.at[quarter_of(m)], s_x3[m], member(m)))
         full = lambda n: mid[n].reshape(skel, skel)
@@ -530,9 +568,9 @@
         for k in reversed(has[2]):
             @pl.when(beside(k)[0])
             def _():
-                q2[k - 1] = dot3(t, full(2 + k), NN)
+                q2[k - 1] = dot_right(t, full(2 + k), NN)
                 q2_copy(k).start()
-        yr2[0] = dot3(t, full(2), NN)
+        yr2[0] = dot_right(t, full(2), NN)
         for k in has[2]:
             phase(f"l2_u{k}")
 
@@ -541,69 +579,95 @@
                 rcopy(q2.at[k - 1], qr2.at[k - 1], s_q2[OPPOSITE[k]], beside(k)[1]).wait_recv()
                 yr2[0] = yr2[0] + qr2[k - 1]
         phase("l2_x")
-        xr = y2[...] - dot3(yr2[0], full(1), NN)
-        xs = t - dot3(xr, full(0), NN)
-        xv = pick_right(jnp.concatenate([xs, xr], axis=1), pick2[...], NT)
-        wide = turned.shape[1]
-        for b in range(4):
-            x2[b] = xv[:, b * wide:(b + 1) * wide]
-        for m in (3, 1, 2):
-            out_copy(m).start()
-        back2[half_of(0), :] = x2[rank[2]]
+        xr = y2[...] - dot_right(yr2[0], full(1), NN)
+        xs = t - dot_right(xr, full(0), NN)
+        x = jnp.concatenate([xs, xr], axis=1)
+        x2[bits[1]] = pick_right(x, pick2[span(bits[1], skel), :], NT)
+        out_copy(1).start()
+        x2[1 - bits[1]] = pick_right(x, pick2[span(1 - bits[1], skel), :], NT)
+        out_copy(3).start()
+        out_copy(2).start()
+        back2[half_of(0), :] = x2[bits[1]]
         phase(None)
 
     phase("l2_out")
-    ptbuf[...] = onehot_p(1)
-    come(rcopy(x2.at[rank[2]], back2.at[half_of(2)], s_x2[2], member(2)), outer)
+    come(rcopy(x2.at[bits[1]], back2.at[half_of(2)], s_x2[2], member(2)), outer)
     for m in (1, 3):
-        come(rcopy(x2.at[rank[2]], back2.at[half_of(m)], s_x2[m], member(m)), inner)
-    t_own = back2[...].T[:skel >> 1]
-
-    for level in (1, 0):
-        phase(f"b{level}_q")
-        cols = skel >> level
-        rows = span(rank[level], cols)
-        s_q = {k: slot() for k in has[level]}
-        for k in along[level] + cross[level]:
-            at_k = pl.ds(k * skel, skel)
-            qsend[level, at_k, :] = dot3(k1[k], t_own, TN) if level else dot3(k0[k], t_own, NN)
-            there, dev = neighbour(level, k)
-            go(rcopy(qsend.at[level, at_k, :], qrecv.at[level, OPPOSITE[k] - 1], s_q[k], dev), there)
-        u = dot3(k1[0], t_own, TN) if level else dot3(k0[0], t_own, NN)
-        phase(f"b{level}_t")
-        if level == 0:
-            abuf[...] = base0[...]
-            abuf[:skel, :] = abuf[:skel, :] + t_own
-            ptbuf[...] = onehot_pt(0)
-        else:
-            abuf[...] = base1[...]
-            abuf[rows, :] = abuf[rows, :] + t_own
-        for k in cross[level] + along[level]:
-            phase(f"b{level}_wait{k}")
-            there, dev = neighbour(level, k)
-            come(rcopy(qsend.at[level, pl.ds(k * skel, skel), :], qrecv.at[level, k - 1], s_q[OPPOSITE[k]], dev), there)
-        phase(f"b{level}_u")
-        u = u + ((qrecv[level, 0] + qrecv[level, 1]) + (qrecv[level, 2] + qrecv[level, 3]))
-        if level > 0:
-            qsend[level, :skel, :] = u
-            c = rcopy(qsend.at[level, span(rank_of(level, 1), cols), :], urecv1.at[0], slot(), member(1))
-            go(c)
-            come(c)
-            u = qsend[level, rows, :] + urecv1[0]
-        phase(f"b{level}_comb")
-        abuf[...] = abuf[...] - (dot3(n1[...], u, TN) if level else dot3(n0[...], u, NN))
-        phase(f"b{level}_x")
-        if level > 0:
-            xpart[...] = pick_left(ptbuf[...], abuf[...], NN)
-            c = rcopy(xpart.at[span(rank_of(level, 1), skel), :], xrecv1.at[0], slot(), member(1))
-            go(c)
-            phase(f"b{level}_xwait")
-            come(c)
-            t_own = xpart[span(rank[level], skel), :] + xrecv1[0]
-        else:
-            ch, cl = halves(abuf[...])
-            pt = ptbuf[...]
-            out[0, 0] = product(ch, pt, TN) + product(cl, pt, TN)
+        come(rcopy(x2.at[bits[1]], back2.at[half_of(m)], s_x2[m], member(m)), inner)
+
+    phase("b1_q")
+    tfull[...] = back2[...].T
+    t_own = tfull[rows, :]
+    others = span(rank_of(1, 1), cols)
+    s_q = {k: slot() for k in has[1]}
+    for k in cross[1]:
+        at_k = pl.ds(k * skel, skel)
+        qsend[1, at_k, :] = dot_left(k1[k], t_own, TN)
+        there, dev = neighbour(1, k)
+        go(rcopy(qsend.at[1, at_k, :], qrecv.at[1, OPPOSITE[k] - 1], s_q[k], dev), there)
+    for k in along[1]:
+        there, dev = neighbour(1, k)
+
+        @pl.when(there)
+        def _():
+            nsend[k - 3] = dot_left(krows[k - 3, 0], t_own, NN) + dot_left(krows[k - 3, 1], tfull[others, :], NN)
+        go(rcopy(nsend.at[k - 3], nrecv.at[OPPOSITE[k] - 3], s_q[k], dev), there)
+    phase("b1_q0")
+    u = dot_left(k1[0], t_own, TN)
+    abuf[...] = base1[...]
+    abuf[rows, :] = abuf[rows, :] + t_own
+    for k in cross[1]:
+        phase(f"b1_wait{k}")
+        there, dev = neighbour(1, k)
+        come(rcopy(qsend.at[1, pl.ds(k * skel, skel), :], qrecv.at[1, k - 1], s_q[OPPOSITE[k]], dev), there)
+        u = u + qrecv[1, k - 1]
+    phase("b1_u")
+    qsend[1, :skel, :] = u
+    give_u = rcopy(qsend.at[1, others, :], urecv1.at[0], slot(), member(1))
+    go(give_u)
+    come(give_u)
+    u = qsend[1, rows, :] + urecv1[0]
+    for k in along[1]:
+        phase(f"b1_wait{k}")
+        there, dev = neighbour(1, k)
+        come(rcopy(nsend.at[k - 3], nrecv.at[k - 3], s_q[OPPOSITE[k]], dev), there)
+        u = u + nrecv[k - 3]
+    phase("b1_comb")
+    abuf[...] = abuf[...] - dot_left(n1[...], u, TN)
+    phase("b1_x")
+    both = jnp.concatenate(halves(abuf[...]), axis=1)
+    for m in (1, 0):
+        spot = span(rank_of(1, m), skel)
+        xpart[spot, :] = lanes_summed(product(ptbuf[spot, :], both, NN))
+        if m:
+            give_x = rcopy(xpart.at[spot, :], xrecv1.at[0], slot(), member(1))
+            go(give_x)
+    phase("b1_xwait")
+    ptbuf[...] = onehot_pt(0)
+    come(give_x)
+    t_own = xpart[span(rank[1], skel), :] + xrecv1[0]
+
+    phase("b0_q")
+    s_q = {k: slot() for k in has[0]}
+    for k in along[0] + cross[0]:
+        at_k = pl.ds(k * skel, skel)
+        qsend[0, at_k, :] = dot_left(k0[k], t_own, NN)
+        there, dev = neighbour(0, k)
+        go(rcopy(qsend.at[0, at_k, :], qrecv.at[0, OPPOSITE[k] - 1], s_q[k], dev), there)
+    u = dot_left(k0[0], t_own, NN)
+    for k in cross[0] + along[0]:
+        phase(f"b0_wait{k}")
+        there, dev = neighbour(0, k)
+        come(rcopy(qsend.at[0, pl.ds(k * skel, skel), :], qrecv.at[0, k - 1], s_q[OPPOSITE[k]], dev), there)
+        u = u + qrecv[0, k - 1]
+    phase("b0_x")
+    xr = ypart[0] - dot_left(g0[...], u, NN)
+    abuf[skel:, :] = xr
+    abuf[:skel, :] = t_own - dot_left(t0[...], xr, NN)
+    phase("b0_out")
+    rhs[...] = pick_right(abuf[...], ptbuf[...], TN)
+    result = pltpu.make_async_copy(rhs, out.at[0, 0], local.at[15])
+    result.start()
 
     phase("drain")
     for when, make in pending:
@@ -635,6 +699,7 @@
             up_copy(m).wait_send()
         for m in (3, 1, 2):
             out_copy(m).wait_send()
+    result.wait()
     phase(None)
 
 
@@ -652,13 +717,15 @@
         vm(rows, box), pltpu.VMEM((4, box), jnp.int32), vm(skel, skel), vm(2, widths[1], skel),
         vm(skel, skel), vm(widths[1], skel), vm(5, skel, skel), vm(5, widths[1], skel),
         vm(2, 5 * skel, rows), vm(box, rows), vm(2, 5 * skel, rows), vm(2, 4, skel, rows),
-        vm(1, widths[1], rows), vm(1, skel, rows), vm(box, rows), vm(box, rows), vm(box, rows),
-        vm(box, skel), vm(widths[1], box),
+        vm(1, widths[1], rows), vm(1, skel, rows), vm(box, rows), vm(box, rows),
+        vm(widths[1], box),
         vm(box, rows), vm(2, skel, rows), vm(1, skel, rows),
         pltpu.VMEM((box, box), BF16), pltpu.VMEM((box, 8), jnp.int32),
+        vm(skel, rows), vm(widths[1], rows), vm(2, widths[1], skel), vm(skel, widths[1]), vm(2, 2, widths[1], widths[1]),
+        vm(skel, rows), vm(2, widths[1], rows), vm(2, widths[1], rows),
         vm(7, 4, widths[2], skel), vm(rows, lanes), vm(4, half, lanes),
         vm(half, skel), vm(4, half, skel), vm(4, half, skel), vm(4, half, skel),
-        vm(4, half, lanes), vm(rows, lanes), pltpu.VMEM((4 * lanes, box), BF16), vm(half, skel), vm(half, skel),
+        vm(2, half, skel), vm(rows, skel), pltpu.VMEM((4 * lanes, box), BF16), vm(half, skel), vm(half, skel),
         vm(3 + kinds, 8, widths[3], skel), vm(2, share, skel),
         vm(share, skel), vm(kinds - 1, share, skel), vm(kinds - 1, share, skel), vm(kinds - 1, share, skel),
         vm(2, share, skel), pltpu.VMEM((box, box), BF16),
@@ -669,12 +736,12 @@
         functools.partial(kernel, size_x, size_y),
         out_shape=jax.ShapeDtypeStruct(right_sides.shape, F32),
         in_specs=[pl.BlockSpec(memory_space=pl.ANY)] * (2 + len(weights)),
-        out_specs=pl.BlockSpec(memory_space=pltpu.VMEM),
+        out_specs=pl.BlockSpec(memory_space=pl.ANY),
         scratch_shapes=scratch,
         compiler_params=pltpu.CompilerParams(
-            collective_id=0, has_side_effects=True, vmem_limit_bytes=60 * 2**20
+            collective_id=0, has_side_effects=True, vmem_limit_bytes=48 * 2**20
         ),
-    )(right_sides, skeleton_order, *weights)
+    )(*[pltpu.with_memory_space_constraint(a, pltpu.HBM) for a in (right_sides, skeleton_order, *weights)])
 
 
 def solution(mesh):

time: 120 us -> 109 us (0.908)
  Pallas kernels: 118 us -> 107 us
    pallas_call x1, Pallas kernels: 118 us -> 107 us  [body(): pl.pallas_call(functools.partial(kernel, size_x, size_y), out_shape=jax.S...]
where the time goes in v4:
time: 109 us; the launch traced here: 108 us
  Pallas kernels  107 us (98%)
    pallas_call x1, Pallas kernels, body(): pl.pallas_call(functools.partial(kernel, size_x, size_y), out_shape=jax.S...  107 us

profile of v4, /device:TPU:1, one launch (start us, length us, event | category | flops | bytes accessed | tf_op | source)
XLA Modules:
  0.0 108.0 jit_solution(10174101023757255243)
XLA Ops:
  0.0 107.2 %shard_map.145 = f32[1,1,128,768]{3,2,1,0:T(8,128)S(1)} custom-call(f32[1,1,128,768]{3,2,1,0:T(8,128)} %refs_0_.1, s32[1,1,4,768]{3,2,1,0:T(4,128)} %refs_1_.1, f32[1,1,384,384]{3,2,1,0:T(8,128)} %refs_2_.1, f32[1,1,192,384]{3,2,1,0:T(8,128)} %bitcast.13, f32[1,1,96,384]{3,2,1,0:T(8,128)} %bitcast.15, f32[1,1,48,384]{3,2,1,0:T(8,128)} %bitcast.17, ...), custom_call_target="tpu_custom_call" | custom-call | tf_op jit(solution)/shard_map/pallas_call | solution.py:735
  107.3 0.7 copy.17

commit v5 on v4

--- a/solution.py
+++ b/solution.py
@@ -64,6 +64,16 @@
     return rows_summed(product(jnp.concatenate(halves(a), axis=0), onehot, dims))
 
 
+def dot_left_of(ah, al, b, dims):
+    bh, bl = halves(b)
+    return lanes_summed(product(ah, jnp.concatenate([bh, bl], axis=1), dims)) + product(al, bh, dims)
+
+
+def dot_right_of(a, bh, bl, dims):
+    ah, al = halves(a)
+    return rows_summed(product(jnp.concatenate([ah, al], axis=0), bh, dims)) + product(ah, bl, dims)
+
+
 class Phases:
     def __init__(self):
         self.scope = None
@@ -80,10 +90,10 @@
     (rhs_in, order_in, t0_in, t1_in, t2_in, t3_in, g0_in, g1_in, g2_in, g3_in,
      k0_in, k1_in, k2_in, k3_in, root_in, out) = refs[:16]
     (rhs, order_row, t0, tg1, g0, g1, k0, k1,
-     ybuf, vbuf, qsend, qrecv, urecv1, xrecv1, xpart, base1,
-     n1, abuf, ypart, ssend, ptbuf, order_col, wbuf, wpart, kmate, kturn, krows, tfull, nsend, nrecv,
-     mid, turned, v2, y2, yr2, q2, qr2, x2, back2, pick2, turn2, t2,
-     top, v3, y3, yr3, q3, qr3, x3, pick3, local, send, recv) = refs[16:]
+     ybuf, vbuf, qsend, qrecv, xrecv1, xpart, base1,
+     abuf, ypart, ssend, ptbuf, order_col, wbuf, wpart, kgive, kturn, krows, tfull, nsend, nrecv,
+     k0h, k0l, n1h, n1l, midh, midl, toph, topl, mid, turned, v2, y2, yr2, q2, qr2, x2, back2, pick2, turn2, t2,
+     top, v3, y3, yr3, q3, qr3, x3, pick3, local, ready, send, recv) = refs[16:]
     skel = t0.shape[0]
     box = 2 * skel
     rhs_count = ybuf.shape[2]
@@ -136,13 +146,25 @@
 
     def go(c, when=None):
         make = c if callable(c) else lambda: c
-        pending.append((when, make))
+        entry = (when, make)
+        pending.append(entry)
         if when is None:
             make().start()
         else:
             @pl.when(when)
             def _():
                 make().start()
+        return entry
+
+    def settle(entries):
+        for when, make in entries:
+            if when is None:
+                make().wait_send()
+            else:
+                @pl.when(when)
+                def _():
+                    make().wait_send()
+        pending[:] = [entry for entry in pending if not any(entry is e for e in entries)]
 
     def come(c, when=None):
         if when is None:
@@ -171,7 +193,7 @@
     load("rhs", rhs_in.at[0, 0], rhs)
     load("t1", t1_in.at[0, 0], tg1.at[rank[1]])
     load("k0", k0_in.at[0, 0], k0)
-    load("g1", g1_in.at[0, 0], g1)
+    load("g1", g1_in.at[0, 0], g1.at[rank[1]])
     load("t2", t2_in.at[0, 0], mid.at[0, rank[2]])
     load("g2", g2_in.at[0, 0], mid.at[1, rank[2]])
     load("k2", k2_in.at[0, 0], mid.at[pl.ds(2, 5), rank[2]])
@@ -216,8 +238,13 @@
     turned[...] = jnp.zeros_like(turned)
 
     chunks = range((top.shape[0] + 1) // 2)
-    slots_own, slots_in, slots_on = ([slot() for _ in chunks] for _ in range(3))
+    slots_in, slots_on = ([slot() for _ in chunks] for _ in range(2))
     slots_mate = [slot() for _ in range(4)]
+    slots_mid = [slot() for _ in range(7)]
+    slots_own = slots_mid[:len(chunks)]
+    among = slots_in + slots_on + slots_mate
+    among = among + [slot() for _ in range(14 - len(among))]
+    slots_mid_own, slots_mid_on = among[:7], among[7:14]
 
     def chunk_copy(c, block, dev, s):
         at = pl.ds(2 * c, min(2, top.shape[0] - 2 * c))
@@ -247,9 +274,6 @@
         go(lambda: mate_copy(n, True), inner)
 
     near = [None, None, None] + [neighbour(2, k)[0] for k in (1, 2, 3, 4)]
-    slots_mid = [slot() for _ in near]
-    slots_mid_own = [slot() for _ in near]
-    slots_mid_on = [slot() for _ in near]
 
     near_in = [inner if there is None else jnp.logical_and(inner, there) for there in near]
     near_out = [outer if there is None else jnp.logical_and(outer, there) for there in near]
@@ -303,29 +327,34 @@
     pl.semaphore_wait(barrier, total)
     phase("f0_send")
     slots_y0 = {k: slot() for k in has[0]}
+    early = []
     for k in along[0] + cross[0]:
         there, dev = neighbour(0, k)
         far = OPPOSITE[k]
-        go(rcopy(ypart.at[0], ybuf.at[0, pl.ds(far * skel, skel), :], slots_y0[k], dev), there)
+        early.append(go(rcopy(ypart.at[0], ybuf.at[0, pl.ds(far * skel, skel), :], slots_y0[k], dev), there))
     need("t2", "g2", "k2", "t3", "g3", "root", "k3")
     mid_send(0)
     outer_send(0)
     inner_send()
     mate_send(0)
+    phase("f0_split")
+    need("k0")
+    for k in range(5):
+        k0h[k], k0l[k] = halves(k0[k])
     phase("f0_s")
-    need("k0")
-    s_own = abuf[:skel, :] - dot_left(k0[0], ypart[0], TN)
+    s_own = abuf[:skel, :] - dot_left_of(k0h[0], k0l[0], ypart[0], TN)
     ptbuf[...] = onehot_pt(1)
     for k in cross[0] + along[0]:
         there, dev = neighbour(0, k)
         phase(f"f0_wait{k}")
         come(rcopy(ypart.at[0], ybuf.at[0, pl.ds(k * skel, skel), :], slots_y0[OPPOSITE[k]], dev), there)
         phase(f"f0_s{k}")
-        s_own = s_own - dot_left(k0[k], ybuf[0, k * skel:(k + 1) * skel, :], TN)
+        s_own = s_own - dot_left_of(k0h[k], k0l[k], ybuf[0, k * skel:(k + 1) * skel, :], TN)
     ssend[0] = s_own
     vbuf[span(rank[1], skel), :] = s_own
-    give = rcopy(ssend.at[0], vbuf.at[span(rank[1], skel), :], slot(), member(1))
-    go(give)
+    s_give = slot()
+    give = rcopy(ssend.at[0], vbuf.at[span(rank[1], skel), :], s_give, member(1))
+    early.append(go(give))
     mid_send(1)
     outer_send(1)
     mid_share(*range(7))
@@ -347,7 +376,7 @@
     phase("f1_wwait")
     come(give_w)
     phase("f1_y")
-    y_own = dot_left(g1[...], wbuf[...], NN)
+    y_own = dot_left(g1[rank[1]], wbuf[...], NN)
     ypart[1, :cols, :] = y_own
     ybuf[1, rows, :] = y_own
 
@@ -364,10 +393,10 @@
     go(mate)
     for k in along[1]:
         there, dev = neighbour(1, k)
-        go(rcopy(own_src, at(OPPOSITE[k], 0), s_b[k], dev), there)
+        early.append(go(rcopy(own_src, at(OPPOSITE[k], 0), s_b[k], dev), there))
     for k in cross[1]:
         there, dev = neighbour(1, k)
-        go(rcopy(own_src, at(OPPOSITE[k], 0), s_c[k][0], dev), there)
+        early.append(go(rcopy(own_src, at(OPPOSITE[k], 0), s_c[k][0], dev), there))
     mid_send(2)
     outer_send(2)
     base1[:skel, :] = -dot_left(tg1[rank[1]], y_own, TN)
@@ -404,17 +433,50 @@
     turned[:, :cols] = s_own.T
 
     phase("l2_send")
-    s_t2 = [slot() for _ in range(4)]
+    s_t2 = {m: slot() for m in (1, 2, 3)}
     half_of = lambda m: span(flipped(1, m), half)
     go(rcopy(turned.at[half_of(1)], v2.at[rank[2]], s_t2[1], member(1)), inner)
     go(rcopy(turned.at[half_of(3)], v2.at[rank[2]], s_t2[3], member(3)), inner)
-    go(rcopy(turned.at[half_of(2)], v2.at[rank[2]], s_t2[2], member(2)), outer)
+    across = go(rcopy(turned.at[half_of(2)], v2.at[rank[2]], s_t2[2], member(2)), outer)
+    pending.pop()
     mid_send(4, 5, 6)
-    t1_copy = rcopy(tg1.at[rank[1]], tg1.at[rank[1]], slot(), member(1))
-    go(t1_copy)
-    mate_k = {k: rcopy(k1.at[k], kmate.at[k - 3], slot(), member(1)) for k in along[1]}
+    s_t1 = [slot(), slot(), slot()]
+    s_k1 = {k: slot() for k in along[1]}
+    near1 = {k: neighbour(1, k)[0] for k in along[1]}
+    near1_in = {k: jnp.logical_and(inner, near1[k]) for k in along[1]}
+    near1_out = {k: jnp.logical_and(outer, near1[k]) for k in along[1]}
+    t1_copy = lambda: rcopy(tg1.at[rank[1]], tg1.at[rank[1]], s_t1[0], member(1))
+    part = cols // 2
+    g1_part = lambda n: g1.at[rank[1], pl.ds(n * part, part), :]
+    g1_copy = lambda n: rcopy(g1_part(n), g1_part(n), s_t1[1 + n], member(1))
+    k1_copy = lambda k: rcopy(kgive.at[k - 3], krows.at[k - 3, 1], s_k1[k], member(1))
+    others = span(rank_of(1, 1), cols)
     for k in along[1]:
-        go(mate_k[k], neighbour(1, k)[0])
+        @pl.when(near1[k])
+        def _():
+            kturn[...] = k1[k].T
+            krows[k - 3, 0] = kturn[rows, :]
+            kgive[k - 3] = kturn[others, :]
+    part = cols // 2
+    g1_part = lambda n: g1.at[rank[1], pl.ds(n * part, part), :]
+    g1_copy = lambda n: rcopy(g1_part(n), g1_part(n), s_t1[1 + n], member(1))
+
+    def late_send(when, near, *wanted):
+        for n in wanted:
+            if n == 3:
+                for k in along[1]:
+                    go(lambda k=k: k1_copy(k), near[k])
+            else:
+                go(t1_copy if n == 0 else lambda n=n: g1_copy(n - 1), when)
+
+    def late_make():
+        come(t1_copy())
+        come(g1_copy(0))
+        come(g1_copy(1))
+        own = g1[...].reshape(skel, skel)
+        n1h[:, :skel], n1l[:, :skel] = halves(-dot3(own, tg1[...].reshape(skel, skel), NN))
+        n1h[:, skel:], n1l[:, skel:] = halves(own)
+
     inner_forward(1)
     inner_forward(2)
 
@@ -431,13 +493,11 @@
             to_i, to_j = i, j + step
         return there, (to_i, to_j)
 
-    s_y2 = {k: slot() for k in has[2]}
-    s_q2 = {k: slot() for k in has[2]}
-    s_t3 = {m: slot() for m in (1, 4)}
-    s_x3 = {m: slot() for m in (1, 4)}
-    s_x2 = {m: slot() for m in (1, 2, 3)}
-    s_y3 = {k: slot() for k in has[3]}
+    s_y2 = s_q2 = {k: slot() for k in has[2]}
+    s_y3 = {k: s_y2[k] for k in has[3]}
     s_q3 = {k: slot() for k in has[3]}
+    s_t3 = s_x3 = {m: slot() for m in (1, 4)}
+    s_x2 = s_t2
     quarter_of = lambda m: span(flipped(2, m), share)
     y2_copy = lambda k: rcopy(y2, yr2.at[OPPOSITE[k] - 1], s_y2[k], beside(k)[1])
     q2_copy = lambda k: rcopy(q2.at[k - 1], qr2.at[OPPOSITE[k] - 1], s_q2[k], beside(k)[1])
@@ -447,29 +507,33 @@
     down_copy = lambda m: rcopy(x3.at[flipped(2, m)], t2.at[quarter_of(0)], s_x3[m], member(m))
     out_copy = lambda m: rcopy(x2.at[flipped(1, m)], back2.at[half_of(0)], s_x2[m], member(m))
 
+    late_send(outer, near1_out, 0)
+
     @pl.when(outer)
     def _():
         phase("l2_pick")
         wide_pick(pick2, 2, cols, turned.shape[1])
         mid_forward(1)
+        full = lambda n: mid[n].reshape(skel, skel)
+        for n in (0, 1):
+            mid_full(n)
+            midh[n], midl[n] = halves(full(n))
         v2[rank[2]] = turned[half_of(0), :]
         phase("l2_in")
         come(rcopy(turned.at[half_of(0)], v2.at[rank_of(2, 2)], s_t2[2], member(2)))
         come(rcopy(turned.at[half_of(0)], v2.at[rank_of(2, 1)], s_t2[1], member(1)))
         come(rcopy(turned.at[half_of(0)], v2.at[rank_of(2, 3)], s_t2[3], member(3)))
         phase("l2_a")
-        full = lambda n: mid[n].reshape(skel, skel)
         a = pick_right(jnp.concatenate([v2[b] for b in range(4)], axis=1), pick2[...], NN)
         s0, r0 = a[:, :skel], a[:, skel:]
         phase("l2_y")
-        mid_full(0)
-        mid_full(1)
-        y = dot_right(r0 - dot_right(s0, full(0), NT), full(1), NT)
+        y = dot_right_of(r0 - dot_right_of(s0, midh[0], midl[0], NT), midh[1], midl[1], NT)
         y2[...] = y
         for k in has[2]:
             @pl.when(beside(k)[0])
             def _():
                 y2_copy(k).start()
+        late_send(outer, near1_out, 1, 2)
         phase("l2_s")
         mid_forward(2)
         mid_full(2)
@@ -486,6 +550,13 @@
                 turn2[...] = turn2[...] - dot_right(yr2[k - 1], full(2 + k), NT)
         for m in (4, 1):
             up_copy(m).start()
+        late_send(outer, near1_out, 3)
+        phase("l2_split")
+        midh[2], midl[2] = halves(full(2))
+        for k in has[2]:
+            @pl.when(beside(k)[0])
+            def _():
+                midh[2 + k], midl[2 + k] = halves(full(2 + k))
         phase(None)
 
     @pl.when(inner)
@@ -496,36 +567,38 @@
             mate_send(n)
         for n in range(4):
             come(mate_copy(n, False))
+        for n in range(3 + kinds):
+            toph[n], topl[n] = halves(top[n].reshape(skel, skel))
         phase("l3_in")
         for m in (1, 4):
             come(rcopy(turn2.at[quarter_of(0)], v3.at[flipped(2, m)], s_t3[m], member(m)))
-        full = lambda n: top[n].reshape(skel, skel)
+        late_send(inner, near1_in, 0, 1)
         phase("l3_y")
         a = pick_right(jnp.concatenate([v3[0], v3[1]], axis=1), pick3[...], NN)
         s0, r0 = a[:, :skel], a[:, skel:]
-        y = dot_right(r0 - dot_right(s0, full(0), NT), full(1), NT)
+        y = dot_right_of(r0 - dot_right_of(s0, toph[0], topl[0], NT), toph[1], topl[1], NT)
         y3[...] = y
         for k in has[3]:
             @pl.when(neighbour(3, k)[0])
             def _():
                 y3_copy(k).start()
         phase("l3_s")
-        v3[0] = s0 - dot_right(y, full(3), NT)
+        v3[0] = s0 - dot_right_of(y, toph[3], topl[3], NT)
         for k in has[3]:
             phase(f"l3_s{k}")
 
             @pl.when(neighbour(3, k)[0])
             def _():
                 rcopy(y3, yr3.at[k - 1], s_y3[OPPOSITE[k]], neighbour(3, k)[1]).wait_recv()
-                v3[0] = v3[0] - dot_right(yr3[k - 1], full(3 + k), NT)
+                v3[0] = v3[0] - dot_right_of(yr3[k - 1], toph[3 + k], topl[3 + k], NT)
         phase("l3_q")
-        t = dot_right(v3[0], full(2), NT)
+        t = dot_right_of(v3[0], toph[2], topl[2], NT)
         for k in has[3]:
             @pl.when(neighbour(3, k)[0])
             def _():
-                q3[k - 1] = dot_right(t, full(3 + k), NN)
+                q3[k - 1] = dot_right_of(t, toph[3 + k], topl[3 + k], NN)
                 q3_copy(k).start()
-        v3[0] = dot_right(t, full(3), NN)
+        v3[0] = dot_right_of(t, toph[3], topl[3], NN)
         for k in has[3]:
             phase(f"l3_u{k}")
 
@@ -534,27 +607,15 @@
                 rcopy(q3.at[k - 1], qr3.at[k - 1], s_q3[OPPOSITE[k]], neighbour(3, k)[1]).wait_recv()
                 v3[0] = v3[0] + qr3[k - 1]
         phase("l3_x")
-        xr = y - dot_right(v3[0], full(1), NN)
-        xs = t - dot_right(xr, full(0), NN)
+        xr = y - dot_right_of(v3[0], toph[1], topl[1], NN)
+        xs = t - dot_right_of(xr, toph[0], topl[0], NN)
         xv = pick_right(jnp.concatenate([xs, xr], axis=1), pick3[...], NT)
         x3[0], x3[1] = xv[:, :skel], xv[:, skel:]
         for m in (4, 1):
             down_copy(m).start()
+        pl.semaphore_wait(ready, 1)
+        late_send(inner, near1_in, 3, 2)
         phase(None)
-
-    phase("b1_make")
-    come(t1_copy)
-    n1[:, :skel] = -dot3(g1[...], tg1[...].reshape(skel, skel), NN)
-    n1[:, skel:] = g1[...]
-    for k in along[1]:
-        there, _ = neighbour(1, k)
-
-        @pl.when(there)
-        def _():
-            mate_k[k].wait_recv()
-            for n, block in enumerate((k1[k], kmate[k - 3])):
-                kturn[...] = block.T
-                krows[k - 3, n] = kturn[rows, :]
 
     @pl.when(outer)
     def _():
@@ -562,15 +623,16 @@
         pick2[:box, :] = onehot_p(2)
         for m in (1, 4):
             come(rcopy(x3.at[bits[2]], t2.at[quarter_of(m)], s_x3[m], member(m)))
-        full = lambda n: mid[n].reshape(skel, skel)
+        pl.semaphore_signal(ready, 1, device_id=member(1), device_id_type=MESH)
         phase("l2_q")
         t = t2[...]
         for k in reversed(has[2]):
             @pl.when(beside(k)[0])
             def _():
-                q2[k - 1] = dot_right(t, full(2 + k), NN)
+                q2[k - 1] = dot_right_of(t, midh[2 + k], midl[2 + k], NN)
+                y2_copy(k).wait_send()
                 q2_copy(k).start()
-        yr2[0] = dot_right(t, full(2), NN)
+        yr2[0] = dot_right_of(t, midh[2], midl[2], NN)
         for k in has[2]:
             phase(f"l2_u{k}")
 
@@ -579,13 +641,14 @@
                 rcopy(q2.at[k - 1], qr2.at[k - 1], s_q2[OPPOSITE[k]], beside(k)[1]).wait_recv()
                 yr2[0] = yr2[0] + qr2[k - 1]
         phase("l2_x")
-        xr = y2[...] - dot_right(yr2[0], full(1), NN)
-        xs = t - dot_right(xr, full(0), NN)
+        xr = y2[...] - dot_right_of(yr2[0], midh[1], midl[1], NN)
+        xs = t - dot_right_of(xr, midh[0], midl[0], NN)
         x = jnp.concatenate([xs, xr], axis=1)
         x2[bits[1]] = pick_right(x, pick2[span(bits[1], skel), :], NT)
         out_copy(1).start()
         x2[1 - bits[1]] = pick_right(x, pick2[span(1 - bits[1], skel), :], NT)
         out_copy(3).start()
+        across[1]().wait_send()
         out_copy(2).start()
         back2[half_of(0), :] = x2[bits[1]]
         phase(None)
@@ -595,11 +658,12 @@
     for m in (1, 3):
         come(rcopy(x2.at[bits[1]], back2.at[half_of(m)], s_x2[m], member(m)), inner)
 
+    phase("b1_settle")
+    settle(early)
     phase("b1_q")
     tfull[...] = back2[...].T
     t_own = tfull[rows, :]
-    others = span(rank_of(1, 1), cols)
-    s_q = {k: slot() for k in has[1]}
+    s_q = {k: s_c[k][0] if k < 3 else s_b[k] for k in has[1]}
     for k in cross[1]:
         at_k = pl.ds(k * skel, skel)
         qsend[1, at_k, :] = dot_left(k1[k], t_own, TN)
@@ -610,37 +674,35 @@
 
         @pl.when(there)
         def _():
+            k1_copy(k).wait_recv()
             nsend[k - 3] = dot_left(krows[k - 3, 0], t_own, NN) + dot_left(krows[k - 3, 1], tfull[others, :], NN)
         go(rcopy(nsend.at[k - 3], nrecv.at[OPPOSITE[k] - 3], s_q[k], dev), there)
     phase("b1_q0")
     u = dot_left(k1[0], t_own, TN)
     abuf[...] = base1[...]
     abuf[rows, :] = abuf[rows, :] + t_own
+    phase("b1_late")
+    late_make()
     for k in cross[1]:
         phase(f"b1_wait{k}")
         there, dev = neighbour(1, k)
         come(rcopy(qsend.at[1, pl.ds(k * skel, skel), :], qrecv.at[1, k - 1], s_q[OPPOSITE[k]], dev), there)
         u = u + qrecv[1, k - 1]
-    phase("b1_u")
     qsend[1, :skel, :] = u
-    give_u = rcopy(qsend.at[1, others, :], urecv1.at[0], slot(), member(1))
-    go(give_u)
-    come(give_u)
-    u = qsend[1, rows, :] + urecv1[0]
     for k in along[1]:
         phase(f"b1_wait{k}")
         there, dev = neighbour(1, k)
         come(rcopy(nsend.at[k - 3], nrecv.at[k - 3], s_q[OPPOSITE[k]], dev), there)
-        u = u + nrecv[k - 3]
+        qsend[1, rows, :] = qsend[1, rows, :] + nrecv[k - 3]
     phase("b1_comb")
-    abuf[...] = abuf[...] - dot_left(n1[...], u, TN)
+    abuf[...] = abuf[...] - dot_left_of(n1h[...], n1l[...], qsend[1, :skel, :], TN)
     phase("b1_x")
     both = jnp.concatenate(halves(abuf[...]), axis=1)
     for m in (1, 0):
         spot = span(rank_of(1, m), skel)
         xpart[spot, :] = lanes_summed(product(ptbuf[spot, :], both, NN))
         if m:
-            give_x = rcopy(xpart.at[spot, :], xrecv1.at[0], slot(), member(1))
+            give_x = rcopy(xpart.at[spot, :], xrecv1.at[0], s_give, member(1))
             go(give_x)
     phase("b1_xwait")
     ptbuf[...] = onehot_pt(0)
@@ -648,13 +710,16 @@
     t_own = xpart[span(rank[1], skel), :] + xrecv1[0]
 
     phase("b0_q")
-    s_q = {k: slot() for k in has[0]}
-    for k in along[0] + cross[0]:
+    s_q = slots_y0
+    for k in cross[0] + along[0]:
         at_k = pl.ds(k * skel, skel)
-        qsend[0, at_k, :] = dot_left(k0[k], t_own, NN)
+        if k % 2:
+            two = slice(k, k + 2)
+            qsend[0, k * skel:(k + 2) * skel, :] = dot_left_of(
+                k0h[two].reshape(2 * skel, skel), k0l[two].reshape(2 * skel, skel), t_own, NN)
         there, dev = neighbour(0, k)
         go(rcopy(qsend.at[0, at_k, :], qrecv.at[0, OPPOSITE[k] - 1], s_q[k], dev), there)
-    u = dot_left(k0[0], t_own, NN)
+    u = dot_left_of(k0h[0], k0l[0], t_own, NN)
     for k in cross[0] + along[0]:
         phase(f"b0_wait{k}")
         there, dev = neighbour(0, k)
@@ -666,9 +731,10 @@
     abuf[:skel, :] = t_own - dot_left(t0[...], xr, NN)
     phase("b0_out")
     rhs[...] = pick_right(abuf[...], ptbuf[...], TN)
-    result = pltpu.make_async_copy(rhs, out.at[0, 0], local.at[15])
+    result = pltpu.make_async_copy(rhs, out.at[0, 0], local.at[0])
     result.start()
 
+    assert count[0] <= send.shape[0], count[0]
     phase("drain")
     for when, make in pending:
         if when is None:
@@ -693,7 +759,6 @@
         for k in has[2]:
             @pl.when(beside(k)[0])
             def _():
-                y2_copy(k).wait_send()
                 q2_copy(k).wait_send()
         for m in (4, 1):
             up_copy(m).wait_send()
@@ -709,28 +774,31 @@
     skel = box // 2
     weights = [jnp.swapaxes(w, -1, -2) if w.shape[-1] < skel else w for w in weights]
     vm = lambda *shape: pltpu.VMEM(shape, F32)
+    half_of = lambda *shape: pltpu.VMEM(shape, BF16)
     widths = [skel >> level for level in range(4)]
     half, share = rows // 2, rows // 4
     kinds = 5 if size_y > REACH[3][1] else 3
+    slots = 49 + kinds
     lanes = -(-widths[1] // 128) * 128
     scratch = [
         vm(rows, box), pltpu.VMEM((4, box), jnp.int32), vm(skel, skel), vm(2, widths[1], skel),
-        vm(skel, skel), vm(widths[1], skel), vm(5, skel, skel), vm(5, widths[1], skel),
+        vm(skel, skel), vm(2, widths[1], skel), vm(5, skel, skel), vm(5, widths[1], skel),
         vm(2, 5 * skel, rows), vm(box, rows), vm(2, 5 * skel, rows), vm(2, 4, skel, rows),
-        vm(1, widths[1], rows), vm(1, skel, rows), vm(box, rows), vm(box, rows),
-        vm(widths[1], box),
+        vm(1, skel, rows), vm(box, rows), vm(box, rows),
         vm(box, rows), vm(2, skel, rows), vm(1, skel, rows),
         pltpu.VMEM((box, box), BF16), pltpu.VMEM((box, 8), jnp.int32),
-        vm(skel, rows), vm(widths[1], rows), vm(2, widths[1], skel), vm(skel, widths[1]), vm(2, 2, widths[1], widths[1]),
+        vm(skel, rows), vm(widths[1], rows), vm(2, widths[1], widths[1]), vm(skel, widths[1]), vm(2, 2, widths[1], widths[1]),
         vm(skel, rows), vm(2, widths[1], rows), vm(2, widths[1], rows),
+        half_of(5, skel, skel), half_of(5, skel, skel), half_of(skel, box), half_of(skel, box),
+        half_of(7, skel, skel), half_of(7, skel, skel), half_of(3 + kinds, skel, skel), half_of(3 + kinds, skel, skel),
         vm(7, 4, widths[2], skel), vm(rows, lanes), vm(4, half, lanes),
         vm(half, skel), vm(4, half, skel), vm(4, half, skel), vm(4, half, skel),
         vm(2, half, skel), vm(rows, skel), pltpu.VMEM((4 * lanes, box), BF16), vm(half, skel), vm(half, skel),
         vm(3 + kinds, 8, widths[3], skel), vm(2, share, skel),
         vm(share, skel), vm(kinds - 1, share, skel), vm(kinds - 1, share, skel), vm(kinds - 1, share, skel),
         vm(2, share, skel), pltpu.VMEM((box, box), BF16),
-        pltpu.SemaphoreType.DMA((16,)),
-        pltpu.SemaphoreType.DMA((128,)), pltpu.SemaphoreType.DMA((128,)),
+        pltpu.SemaphoreType.DMA((15,)), pltpu.SemaphoreType.REGULAR,
+        pltpu.SemaphoreType.DMA((slots,)), pltpu.SemaphoreType.DMA((slots,)),
     ]
     return pl.pallas_call(
         functools.partial(kernel, size_x, size_y),

time: 109 us -> 103 us (0.945)
  Pallas kernels: 107 us -> 102 us
    pallas_call x1, Pallas kernels: 107 us -> 102 us  [body(): pl.pallas_call(functools.partial(kernel, size_x, size_y), out_shape=jax.S...]
where the time goes in v5:
time: 103 us; the launch traced here: 102 us
  Pallas kernels  102 us (99%)
    pallas_call x1, Pallas kernels, body(): pl.pallas_call(functools.partial(kernel, size_x, size_y), out_shape=jax.S...  102 us

profile of v5, /device:TPU:1, one launch (start us, length us, event | category | flops | bytes accessed | tf_op | source)
XLA Modules:
  0.0 102.5 jit_solution(15260466390964447557)
XLA Ops:
  0.0 101.7 %shard_map.145 = f32[1,1,128,768]{3,2,1,0:T(8,128)S(1)} custom-call(f32[1,1,128,768]{3,2,1,0:T(8,128)} %refs_0_.1, s32[1,1,4,768]{3,2,1,0:T(4,128)} %refs_1_.1, f32[1,1,384,384]{3,2,1,0:T(8,128)} %refs_2_.1, f32[1,1,192,384]{3,2,1,0:T(8,128)} %bitcast.13, f32[1,1,96,384]{3,2,1,0:T(8,128)} %bitcast.15, f32[1,1,48,384]{3,2,1,0:T(8,128)} %bitcast.17, ...), custom_call_target="tpu_custom_call" | custom-call | tf_op jit(solution)/shard_map/pallas_call | solution.py:803
  101.7 0.7 copy.17

commit v6 on v5

--- a/solution.py
+++ b/solution.py
@@ -93,7 +93,7 @@
      ybuf, vbuf, qsend, qrecv, xrecv1, xpart, base1,
      abuf, ypart, ssend, ptbuf, order_col, wbuf, wpart, kgive, kturn, krows, tfull, nsend, nrecv,
      k0h, k0l, n1h, n1l, midh, midl, toph, topl, mid, turned, v2, y2, yr2, q2, qr2, x2, back2, pick2, turn2, t2,
-     top, v3, y3, yr3, q3, qr3, x3, pick3, local, ready, send, recv) = refs[16:]
+     top, v3, y3, yr3, q3, qr3, x3, pick3, pair, pairh, pairl, yq, x3n, qn2, local, ready, send, recv) = refs[16:]
     skel = t0.shape[0]
     box = 2 * skel
     rhs_count = ybuf.shape[2]
@@ -197,6 +197,7 @@
     load("t2", t2_in.at[0, 0], mid.at[0, rank[2]])
     load("g2", g2_in.at[0, 0], mid.at[1, rank[2]])
     load("k2", k2_in.at[0, 0], mid.at[pl.ds(2, 5), rank[2]])
+    load("kn", k2_in.at[0, 0, 4 - bits[2]], pair.at[rank[3]])
     load("t3", t3_in.at[0, 0], top.at[0, rank[3]])
     load("g3", g3_in.at[0, 0], top.at[1, rank[3]])
     load("root", root_in.at[0, 0], top.at[2, rank[3]])
@@ -238,15 +239,19 @@
     turned[...] = jnp.zeros_like(turned)
 
     chunks = range((top.shape[0] + 1) // 2)
-    slots_in, slots_on = ([slot() for _ in chunks] for _ in range(2))
+    last = len(chunks)
+    slots_in, slots_on = ([slot() for _ in range(last + 1)] for _ in range(2))
     slots_mate = [slot() for _ in range(4)]
+    slots_pair = [slot() for _ in range(4)]
     slots_mid = [slot() for _ in range(7)]
-    slots_own = slots_mid[:len(chunks)]
-    among = slots_in + slots_on + slots_mate
+    slots_own = slots_mid[:last + 1]
+    among = slots_in + slots_on + slots_mate + slots_pair
     among = among + [slot() for _ in range(14 - len(among))]
     slots_mid_own, slots_mid_on = among[:7], among[7:14]
 
     def chunk_copy(c, block, dev, s):
+        if c == last:
+            return rcopy(pair.at[block], pair.at[block], s, dev)
         at = pl.ds(2 * c, min(2, top.shape[0] - 2 * c))
         return rcopy(top.at[at, block], top.at[at, block], s, dev)
 
@@ -254,11 +259,15 @@
         block = rank_of(3, (0, 1, 5, 4)[n] ^ (0 if mine else 2))
         return rcopy(top.at[:, block], top.at[:, block], slots_mate[n], member(2))
 
+    def pair_copy(n, mine):
+        block = rank_of(3, (0, 1, 5, 4)[n] ^ (0 if mine else 2))
+        return rcopy(pair.at[block], pair.at[block], slots_pair[n], member(2))
+
     def outer_send(c):
         go(chunk_copy(c, rank[3], member(1), slots_own[c]), outer)
 
     def inner_send():
-        for c in chunks:
+        for c in range(last + 1):
             go(chunk_copy(c, rank[3], member(5), slots_in[c]), inner)
 
     def inner_forward(c):
@@ -266,14 +275,17 @@
         go(chunk_copy(c, rank_of(3, 1), member(5), slots_on[c]), inner)
 
     def mate_send(n):
-        for c in chunks:
+        for c in range(last + 1):
             if n == 2:
                 come(chunk_copy(c, rank_of(3, 5), member(5), slots_in[c]), inner)
             if n == 3:
                 come(chunk_copy(c, rank_of(3, 4), member(5), slots_on[c]), inner)
         go(lambda: mate_copy(n, True), inner)
-
-    near = [None, None, None] + [neighbour(2, k)[0] for k in (1, 2, 3, 4)]
+        go(lambda: pair_copy(n, True), inner)
+
+    sides = cross[2] + (along[2] if size_y > REACH[3][1] else [])
+    near = [None, None, None] + [neighbour(2, k)[0] for k in (1, 2)] + [
+        jnp.logical_and(neighbour(2, 3)[0], bits[2] == 0), jnp.logical_and(neighbour(2, 4)[0], bits[2] == 1)]
 
     near_in = [inner if there is None else jnp.logical_and(inner, there) for there in near]
     near_out = [outer if there is None else jnp.logical_and(outer, there) for there in near]
@@ -283,7 +295,7 @@
         return rcopy(mid.at[n, block], mid.at[n, block], s, member(to))
 
     def used(n):
-        return n < 3 or n - 2 in has[2]
+        return n < 3 or n - 2 in sides
 
     def mid_send(*wanted):
         for n in filter(used, wanted):
@@ -332,7 +344,7 @@
         there, dev = neighbour(0, k)
         far = OPPOSITE[k]
         early.append(go(rcopy(ypart.at[0], ybuf.at[0, pl.ds(far * skel, skel), :], slots_y0[k], dev), there))
-    need("t2", "g2", "k2", "t3", "g3", "root", "k3")
+    need("t2", "g2", "k2", "kn", "t3", "g3", "root", "k3")
     mid_send(0)
     outer_send(0)
     inner_send()
@@ -440,6 +452,7 @@
     across = go(rcopy(turned.at[half_of(2)], v2.at[rank[2]], s_t2[2], member(2)), outer)
     pending.pop()
     mid_send(4, 5, 6)
+    outer_send(last)
     s_t1 = [slot(), slot(), slot()]
     s_k1 = {k: slot() for k in along[1]}
     near1 = {k: neighbour(1, k)[0] for k in along[1]}
@@ -479,6 +492,7 @@
 
     inner_forward(1)
     inner_forward(2)
+    inner_forward(last)
 
     def wide_pick(pick, level, width, lanes):
         o = order_row[level:level + 1, :]
@@ -487,13 +501,10 @@
         pick[...] = jnp.where(lines == o, 1.0, 0.0).astype(BF16)
 
     def beside(k):
-        there, (to_i, to_j) = neighbour(2, k)
-        if k > 2:
-            step = 1 + 2 * (1 - bits[2]) if k == 4 else -(1 + 2 * bits[2])
-            to_i, to_j = i, j + step
-        return there, (to_i, to_j)
-
-    s_y2 = s_q2 = {k: slot() for k in has[2]}
+        to = neighbour(2, k)[1] if k < 3 else (i, j + 1 if k == 4 else j - 1)
+        return near[2 + k], to
+
+    s_y2 = s_q2 = {k: slot() for k in sides}
     s_y3 = {k: s_y2[k] for k in has[3]}
     s_q3 = {k: slot() for k in has[3]}
     s_t3 = s_x3 = {m: slot() for m in (1, 4)}
@@ -503,11 +514,13 @@
     q2_copy = lambda k: rcopy(q2.at[k - 1], qr2.at[OPPOSITE[k] - 1], s_q2[k], beside(k)[1])
     y3_copy = lambda k: rcopy(y3, yr3.at[OPPOSITE[k] - 1], s_y3[k], neighbour(3, k)[1])
     q3_copy = lambda k: rcopy(q3.at[k - 1], qr3.at[OPPOSITE[k] - 1], s_q3[k], neighbour(3, k)[1])
+    s_yq = {1: slots_mid[5], 4: slots_mid[6]}
+    s_qn = {m: slot() for m in (1, 4)}
+    yq_copy = lambda m: rcopy(y2.at[quarter_of(m)], yq.at[bits[2]], s_yq[m], member(m))
+    qn_copy = lambda m: rcopy(x3n.at[flipped(2, m)], qn2.at[quarter_of(0)], s_qn[m], member(m))
     up_copy = lambda m: rcopy(turn2.at[quarter_of(m)], v3.at[bits[2]], s_t3[m], member(m))
     down_copy = lambda m: rcopy(x3.at[flipped(2, m)], t2.at[quarter_of(0)], s_x3[m], member(m))
     out_copy = lambda m: rcopy(x2.at[flipped(1, m)], back2.at[half_of(0)], s_x2[m], member(m))
-
-    late_send(outer, near1_out, 0)
 
     @pl.when(outer)
     def _():
@@ -529,18 +542,19 @@
         phase("l2_y")
         y = dot_right_of(r0 - dot_right_of(s0, midh[0], midl[0], NT), midh[1], midl[1], NT)
         y2[...] = y
-        for k in has[2]:
+        for m in (4, 1):
+            yq_copy(m).start()
+        for k in sides:
             @pl.when(beside(k)[0])
             def _():
                 y2_copy(k).start()
-        late_send(outer, near1_out, 1, 2)
         phase("l2_s")
         mid_forward(2)
         mid_full(2)
         turn2[...] = s0 - dot_right(y, full(2), NT)
-        for k in has[2]:
+        for k in sides:
             mid_forward(2 + k)
-        for k in has[2]:
+        for k in sides:
             phase(f"l2_s{k}")
 
             @pl.when(beside(k)[0])
@@ -550,10 +564,10 @@
                 turn2[...] = turn2[...] - dot_right(yr2[k - 1], full(2 + k), NT)
         for m in (4, 1):
             up_copy(m).start()
-        late_send(outer, near1_out, 3)
+        late_send(outer, near1_out, 0, 1, 2, 3)
         phase("l2_split")
         midh[2], midl[2] = halves(full(2))
-        for k in has[2]:
+        for k in sides:
             @pl.when(beside(k)[0])
             def _():
                 midh[2 + k], midl[2 + k] = halves(full(2 + k))
@@ -567,14 +581,22 @@
             mate_send(n)
         for n in range(4):
             come(mate_copy(n, False))
+            come(pair_copy(n, False))
         for n in range(3 + kinds):
             toph[n], topl[n] = halves(top[n].reshape(skel, skel))
+        for n in range(2):
+            pairh[n], pairl[n] = halves(pair[4 * n:4 * n + 4].reshape(skel, skel))
+        phase("l3_pair")
+        for m in (1, 4):
+            come(rcopy(y2.at[quarter_of(0)], yq.at[flipped(2, m)], s_yq[m], member(m)))
+        for n in range(2):
+            x3n[n] = dot_right_of(yq[1 - n], pairh[n], pairl[n], NT)
         phase("l3_in")
         for m in (1, 4):
             come(rcopy(turn2.at[quarter_of(0)], v3.at[flipped(2, m)], s_t3[m], member(m)))
         late_send(inner, near1_in, 0, 1)
         phase("l3_y")
-        a = pick_right(jnp.concatenate([v3[0], v3[1]], axis=1), pick3[...], NN)
+        a = pick_right(jnp.concatenate([v3[0] - x3n[0], v3[1] - x3n[1]], axis=1), pick3[...], NN)
         s0, r0 = a[:, :skel], a[:, skel:]
         y = dot_right_of(r0 - dot_right_of(s0, toph[0], topl[0], NT), toph[1], topl[1], NT)
         y3[...] = y
@@ -613,6 +635,10 @@
         x3[0], x3[1] = xv[:, :skel], xv[:, skel:]
         for m in (4, 1):
             down_copy(m).start()
+        for n in range(2):
+            x3n[1 - n] = dot_right_of(x3[n], pairh[n], pairl[n], NN)
+        for m in (4, 1):
+            qn_copy(m).start()
         pl.semaphore_wait(ready, 1)
         late_send(inner, near1_in, 3, 2)
         phase(None)
@@ -626,20 +652,24 @@
         pl.semaphore_signal(ready, 1, device_id=member(1), device_id_type=MESH)
         phase("l2_q")
         t = t2[...]
-        for k in reversed(has[2]):
+        for k in reversed(sides):
             @pl.when(beside(k)[0])
             def _():
                 q2[k - 1] = dot_right_of(t, midh[2 + k], midl[2 + k], NN)
                 y2_copy(k).wait_send()
                 q2_copy(k).start()
         yr2[0] = dot_right_of(t, midh[2], midl[2], NN)
-        for k in has[2]:
+        for k in sides:
             phase(f"l2_u{k}")
 
             @pl.when(beside(k)[0])
             def _():
                 rcopy(q2.at[k - 1], qr2.at[k - 1], s_q2[OPPOSITE[k]], beside(k)[1]).wait_recv()
                 yr2[0] = yr2[0] + qr2[k - 1]
+        phase("l2_qn")
+        for m in (1, 4):
+            come(rcopy(x3n.at[bits[2]], qn2.at[quarter_of(m)], s_qn[m], member(m)))
+        yr2[0] = yr2[0] + qn2[...]
         phase("l2_x")
         xr = y2[...] - dot_right_of(yr2[0], midh[1], midl[1], NN)
         xs = t - dot_right_of(xr, midh[0], midl[0], NN)
@@ -753,15 +783,17 @@
                 q3_copy(k).wait_send()
         for m in (4, 1):
             down_copy(m).wait_send()
+            qn_copy(m).wait_send()
 
     @pl.when(outer)
     def _():
-        for k in has[2]:
+        for k in sides:
             @pl.when(beside(k)[0])
             def _():
                 q2_copy(k).wait_send()
         for m in (4, 1):
             up_copy(m).wait_send()
+            yq_copy(m).wait_send()
         for m in (3, 1, 2):
             out_copy(m).wait_send()
     result.wait()
@@ -778,7 +810,7 @@
     widths = [skel >> level for level in range(4)]
     half, share = rows // 2, rows // 4
     kinds = 5 if size_y > REACH[3][1] else 3
-    slots = 49 + kinds
+    slots = 54 if kinds == 3 else 60
     lanes = -(-widths[1] // 128) * 128
     scratch = [
         vm(rows, box), pltpu.VMEM((4, box), jnp.int32), vm(skel, skel), vm(2, widths[1], skel),
@@ -797,7 +829,8 @@
         vm(3 + kinds, 8, widths[3], skel), vm(2, share, skel),
         vm(share, skel), vm(kinds - 1, share, skel), vm(kinds - 1, share, skel), vm(kinds - 1, share, skel),
         vm(2, share, skel), pltpu.VMEM((box, box), BF16),
-        pltpu.SemaphoreType.DMA((15,)), pltpu.SemaphoreType.REGULAR,
+        vm(8, widths[2], skel), half_of(2, skel, skel), half_of(2, skel, skel), vm(2, share, skel), vm(2, share, skel), vm(half, skel),
+        pltpu.SemaphoreType.DMA((16,)), pltpu.SemaphoreType.REGULAR,
         pltpu.SemaphoreType.DMA((slots,)), pltpu.SemaphoreType.DMA((slots,)),
     ]
     return pl.pallas_call(
@@ -807,7 +840,7 @@
         out_specs=pl.BlockSpec(memory_space=pl.ANY),
         scratch_shapes=scratch,
         compiler_params=pltpu.CompilerParams(
-            collective_id=0, has_side_effects=True, vmem_limit_bytes=48 * 2**20
+            collective_id=0, has_side_effects=True, vmem_limit_bytes=(48 if kinds == 3 else 58) * 2**20
         ),
     )(*[pltpu.with_memory_space_constraint(a, pltpu.HBM) for a in (right_sides, skeleton_order, *weights)])
 

time: 103 us -> 100 us (0.971)
  Pallas kernels: 102 us -> 98.9 us
    pallas_call x1, Pallas kernels: 102 us -> 98.9 us  [body(): pl.pallas_call(functools.partial(kernel, size_x, size_y), out_shape=jax.S...]
where the time goes in v6:
time: 100 us; the launch traced here: 99.7 us
  Pallas kernels  98.9 us (99%)
    pallas_call x1, Pallas kernels, body(): pl.pallas_call(functools.partial(kernel, size_x, size_y), out_shape=jax.S...  98.9 us

profile of v6, /device:TPU:1, one launch (start us, length us, event | category | flops | bytes accessed | tf_op | source)
XLA Modules:
  0.0 99.7 jit_solution(15735486165786365938)
XLA Ops:
  0.0 98.9 %shard_map.145 = f32[1,1,128,768]{3,2,1,0:T(8,128)S(1)} custom-call(f32[1,1,128,768]{3,2,1,0:T(8,128)} %refs_0_.1, s32[1,1,4,768]{3,2,1,0:T(4,128)} %refs_1_.1, f32[1,1,384,384]{3,2,1,0:T(8,128)} %refs_2_.1, f32[1,1,192,384]{3,2,1,0:T(8,128)} %bitcast.13, f32[1,1,96,384]{3,2,1,0:T(8,128)} %bitcast.15, f32[1,1,48,384]{3,2,1,0:T(8,128)} %bitcast.17, ...), custom_call_target="tpu_custom_call" | custom-call | tf_op jit(solution)/shard_map/pallas_call | solution.py:836
  98.9 0.7 copy.17

commit v7 on v6

--- a/solution.py
+++ b/solution.py
@@ -91,8 +91,8 @@
      k0_in, k1_in, k2_in, k3_in, root_in, out) = refs[:16]
     (rhs, order_row, t0, tg1, g0, g1, k0, k1,
      ybuf, vbuf, qsend, qrecv, xrecv1, xpart, base1,
-     abuf, ypart, ssend, ptbuf, order_col, wbuf, wpart, kgive, kturn, krows, tfull, nsend, nrecv,
-     k0h, k0l, n1h, n1l, midh, midl, toph, topl, mid, turned, v2, y2, yr2, q2, qr2, x2, back2, pick2, turn2, t2,
+     abuf, ypart, ssend, ptbuf, order_col, wbuf, wpart, kgive, kturn, krows, kch, kcl, tfull, nsend, nrecv,
+     k0h, k0l, n0h, n0l, base0, n1h, n1l, midh, midl, toph, topl, mid, turned, v2, y2, yr2, q2, qr2, x2, back2, pick2, turn2, t2,
      top, v3, y3, yr3, q3, qr3, x3, pick3, pair, pairh, pairl, yq, x3n, qn2, local, ready, send, recv) = refs[16:]
     skel = t0.shape[0]
     box = 2 * skel
@@ -221,22 +221,6 @@
             def _():
                 pl.semaphore_signal(barrier, 1, device_id=dev, device_id_type=MESH)
             total = total + there.astype(jnp.int32)
-
-    for level in range(2):
-        for k in (1, 2, 3, 4):
-            there, _ = neighbour(level, k)
-
-            @pl.when(jnp.logical_not(there))
-            def _():
-                ybuf[level, k * skel:(k + 1) * skel, :] = jnp.zeros((skel, rhs_count), F32)
-                qrecv[level, k - 1] = jnp.zeros((skel, rhs_count), F32)
-    for k in along[1]:
-        there, _ = neighbour(1, k)
-
-        @pl.when(jnp.logical_not(there))
-        def _():
-            nrecv[k - 3] = jnp.zeros(nrecv.shape[1:], F32)
-    turned[...] = jnp.zeros_like(turned)
 
     chunks = range((top.shape[0] + 1) // 2)
     last = len(chunks)
@@ -344,6 +328,21 @@
         there, dev = neighbour(0, k)
         far = OPPOSITE[k]
         early.append(go(rcopy(ypart.at[0], ybuf.at[0, pl.ds(far * skel, skel), :], slots_y0[k], dev), there))
+    for level in range(2):
+        for k in (1, 2, 3, 4):
+            there, _ = neighbour(level, k)
+
+            @pl.when(jnp.logical_not(there))
+            def _():
+                ybuf[level, k * skel:(k + 1) * skel, :] = jnp.zeros((skel, rhs_count), F32)
+                qrecv[level, k - 1] = jnp.zeros((skel, rhs_count), F32)
+    for k in along[1]:
+        there, _ = neighbour(1, k)
+
+        @pl.when(jnp.logical_not(there))
+        def _():
+            nrecv[k - 3] = jnp.zeros(nrecv.shape[1:], F32)
+    turned[...] = jnp.zeros_like(turned)
     need("t2", "g2", "k2", "kn", "t3", "g3", "root", "k3")
     mid_send(0)
     outer_send(0)
@@ -370,6 +369,8 @@
     mid_send(1)
     outer_send(1)
     mid_share(*range(7))
+    halves_at = [span(rank_of(1, m), skel) for m in (0, 1)]
+    abuf[...] = pick_left(ptbuf[:, halves_at[0]], ssend[0], NN)
     phase("f0_gwait")
     need("t1", "g1", "k1")
     come(give)
@@ -377,7 +378,7 @@
     phase("f1_a")
     cols = skel >> 1
     rows = span(rank[1], cols)
-    abuf[...] = pick_left(ptbuf[...], vbuf[...], NN)
+    abuf[...] = abuf[...] + pick_left(ptbuf[:, halves_at[1]], vbuf[halves_at[1], :], NN)
     phase("f1_w")
     w_own = abuf[pl.ds(pl.multiple_of(skel + rank[1] * cols, cols), cols), :] - dot_left(tg1[rank[1]], abuf[:skel, :], NN)
     wpart[...] = w_own
@@ -459,6 +460,8 @@
     near1_in = {k: jnp.logical_and(inner, near1[k]) for k in along[1]}
     near1_out = {k: jnp.logical_and(outer, near1[k]) for k in along[1]}
     t1_copy = lambda: rcopy(tg1.at[rank[1]], tg1.at[rank[1]], s_t1[0], member(1))
+    if cross[1]:
+        kch[...], kcl[...] = halves(jnp.concatenate([k1[1], k1[2]], axis=1))
     part = cols // 2
     g1_part = lambda n: g1.at[rank[1], pl.ds(n * part, part), :]
     g1_copy = lambda n: rcopy(g1_part(n), g1_part(n), s_t1[1 + n], member(1))
@@ -521,6 +524,11 @@
     up_copy = lambda m: rcopy(turn2.at[quarter_of(m)], v3.at[bits[2]], s_t3[m], member(m))
     down_copy = lambda m: rcopy(x3.at[flipped(2, m)], t2.at[quarter_of(0)], s_x3[m], member(m))
     out_copy = lambda m: rcopy(x2.at[flipped(1, m)], back2.at[half_of(0)], s_x2[m], member(m))
+
+    def make_n0():
+        n0h[:skel, :], n0l[:skel, :] = halves(-dot3(t0[...], g0[...], NN))
+        n0h[skel:, :], n0l[skel:, :] = halves(g0[...])
+        base0[...] = -dot_left(t0[...], ypart[0], NN)
 
     @pl.when(outer)
     def _():
@@ -571,10 +579,13 @@
             @pl.when(beside(k)[0])
             def _():
                 midh[2 + k], midl[2 + k] = halves(full(2 + k))
+        make_n0()
         phase(None)
 
     @pl.when(inner)
     def _():
+        phase("l3_n0")
+        make_n0()
         phase("l3_pick")
         wide_pick(pick3, 3, skel, skel)
         for n in (1, 2, 3):
@@ -694,9 +705,9 @@
     tfull[...] = back2[...].T
     t_own = tfull[rows, :]
     s_q = {k: s_c[k][0] if k < 3 else s_b[k] for k in has[1]}
+    qsend[1, skel:3 * skel, :] = dot_left_of(kch[...], kcl[...], t_own, TN)
     for k in cross[1]:
         at_k = pl.ds(k * skel, skel)
-        qsend[1, at_k, :] = dot_left(k1[k], t_own, TN)
         there, dev = neighbour(1, k)
         go(rcopy(qsend.at[1, at_k, :], qrecv.at[1, OPPOSITE[k] - 1], s_q[k], dev), there)
     for k in along[1]:
@@ -750,15 +761,15 @@
         there, dev = neighbour(0, k)
         go(rcopy(qsend.at[0, at_k, :], qrecv.at[0, OPPOSITE[k] - 1], s_q[k], dev), there)
     u = dot_left_of(k0h[0], k0l[0], t_own, NN)
+    abuf[:skel, :] = base0[...] + t_own
+    abuf[skel:, :] = ypart[0]
     for k in cross[0] + along[0]:
         phase(f"b0_wait{k}")
         there, dev = neighbour(0, k)
         come(rcopy(qsend.at[0, pl.ds(k * skel, skel), :], qrecv.at[0, k - 1], s_q[OPPOSITE[k]], dev), there)
         u = u + qrecv[0, k - 1]
     phase("b0_x")
-    xr = ypart[0] - dot_left(g0[...], u, NN)
-    abuf[skel:, :] = xr
-    abuf[:skel, :] = t_own - dot_left(t0[...], xr, NN)
+    abuf[...] = abuf[...] - dot_left_of(n0h[...], n0l[...], u, NN)
     phase("b0_out")
     rhs[...] = pick_right(abuf[...], ptbuf[...], TN)
     result = pltpu.make_async_copy(rhs, out.at[0, 0], local.at[0])
@@ -819,9 +830,9 @@
         vm(1, skel, rows), vm(box, rows), vm(box, rows),
         vm(box, rows), vm(2, skel, rows), vm(1, skel, rows),
         pltpu.VMEM((box, box), BF16), pltpu.VMEM((box, 8), jnp.int32),
-        vm(skel, rows), vm(widths[1], rows), vm(2, widths[1], widths[1]), vm(skel, widths[1]), vm(2, 2, widths[1], widths[1]),
+        vm(skel, rows), vm(widths[1], rows), vm(2, widths[1], widths[1]), vm(skel, widths[1]), vm(2, 2, widths[1], widths[1]), half_of(widths[1], box), half_of(widths[1], box),
         vm(skel, rows), vm(2, widths[1], rows), vm(2, widths[1], rows),
-        half_of(5, skel, skel), half_of(5, skel, skel), half_of(skel, box), half_of(skel, box),
+        half_of(5, skel, skel), half_of(5, skel, skel), half_of(box, skel), half_of(box, skel), vm(skel, rows), half_of(skel, box), half_of(skel, box),
         half_of(7, skel, skel), half_of(7, skel, skel), half_of(3 + kinds, skel, skel), half_of(3 + kinds, skel, skel),
         vm(7, 4, widths[2], skel), vm(rows, lanes), vm(4, half, lanes),
         vm(half, skel), vm(4, half, skel), vm(4, half, skel), vm(4, half, skel),
@@ -840,7 +851,7 @@
         out_specs=pl.BlockSpec(memory_space=pl.ANY),
         scratch_shapes=scratch,
         compiler_params=pltpu.CompilerParams(
-            collective_id=0, has_side_effects=True, vmem_limit_bytes=(48 if kinds == 3 else 58) * 2**20
+            collective_id=0, has_side_effects=True, vmem_limit_bytes=(52 if kinds == 3 else 62) * 2**20
         ),
     )(*[pltpu.with_memory_space_constraint(a, pltpu.HBM) for a in (right_sides, skeleton_order, *weights)])
 

time: 100 us -> 101 us (1.010); the launches traced: 99.7 us -> 99.4 us
  no operation moved by 1% of the time
where the time goes in v7:
time: 101 us; the launch traced here: 99.4 us
  Pallas kernels  98.6 us (98%)
    pallas_call x1, Pallas kernels, body(): pl.pallas_call(functools.partial(kernel, size_x, size_y), out_shape=jax.S...  98.6 us

profile of v7, /device:TPU:1, one launch (start us, length us, event | category | flops | bytes accessed | tf_op | source)
XLA Modules:
  0.0 99.4 jit_solution(11656235918368582966)
XLA Ops:
  0.0 98.6 %shard_map.145 = f32[1,1,128,768]{3,2,1,0:T(8,128)S(1)} custom-call(f32[1,1,128,768]{3,2,1,0:T(8,128)} %refs_0_.1, s32[1,1,4,768]{3,2,1,0:T(4,128)} %refs_1_.1, f32[1,1,384,384]{3,2,1,0:T(8,128)} %refs_2_.1, f32[1,1,192,384]{3,2,1,0:T(8,128)} %bitcast.13, f32[1,1,96,384]{3,2,1,0:T(8,128)} %bitcast.15, f32[1,1,48,384]{3,2,1,0:T(8,128)} %bitcast.17, ...), custom_call_target="tpu_custom_call" | custom-call | tf_op jit(solution)/shard_map/pallas_call | solution.py:847
  98.6 0.7 copy.17
